TPU v7x, 256 devices: a whole 4x4x8 slice. The times are simulated.
256 devices in a mesh: chan: 32 (over y, x, core), head: 4 (over z_lo), region: 2 (over z_hi).
Axes of the slice: x: 4, y: 4, z: 8 (z_hi: 2, z_lo: 4; z = z_hi * 4 + z_lo), core: 2. Of those that a mesh axis runs over, the one named last changes fastest.
Arguments:
- tokens: bfloat16 [512, 16, 4096], P('chan', 'region', 'head'), parts along dimension 1, may hold values from -56 to 56
- position: bfloat16 [512, 4096], P('chan', 'head'), may hold values from -3 to 3
- gain: bfloat16 [4096], P('head'), may hold values from 0.099609375 to 1.8984375
- qkv_weight: bfloat16 [3, 4096, 2048], P(None, 'chan', 'head'), may hold values from -0.09375 to 0.09375
- out_weight: bfloat16 [2048, 4096], P('head'), may hold values from -0.25 to 0.25
- cotangent: bfloat16 [512, 16, 4096], P('chan', 'region', 'head'), parts along dimension 1, may hold values from -6 to 6
Outputs:
- layer_out: bfloat16 [512, 16, 4096], P('chan', 'region', 'head'), parts along dimension 1
- input_grad: bfloat16 [512, 16, 4096], P('chan', 'region', 'head'), parts along dimension 1
There are 2 independent parts, one for each index of `region`. A program takes and returns all parts, laid end to end along the dimension named above; an argument that names none is the same for every part. Nothing has to cross between parts.
All inputs are finite; a program needn't handle non-finite values.
Results may differ from a plain program's by a relative error of at most 0.01.
Values may be sent and summed in bfloat16 or wider, within the bound.
No kernel may reach another device: no remote copies, remote signals or barrier semaphores. Data moves between devices by JAX's collectives and lax.ppermute only.
A program may use at most 64 MiB of HBM per device.

v0:
```python
import jax
import jax.numpy as jnp
from jax import lax
from jax.experimental import pallas as pl
from jax.experimental.pallas import tpu as pltpu
from jax.sharding import PartitionSpec as P


F32 = jnp.float32
BF = jnp.bfloat16
NY, NX, NC, NZ = 4, 4, 2, 4
HD = 128
FAC = HD ** -0.5
CHG = 16
PAT = 8


def chan_id(y, x, c):
    return (y % NY) * (NX * NC) + (x % NX) * NC + (c % NC)


SITES = [(y, x, c) for y in range(NY) for x in range(NX) for c in range(NC)]
SWAP = [(chan_id(y, x, c), chan_id(y, x, c + 1)) for y, x, c in SITES]
SAME_CORE = [[chan_id(y, x, c) for y in range(NY) for x in range(NX)] for c in range(NC)]


def ring(first, step):
    pairs = []
    for y, x, c in SITES:
        if (c == 0) == first:
            pairs.append((chan_id(y, x, c), chan_id(y, x + step, c)))
        else:
            pairs.append((chan_id(y, x, c), chan_id(y + step, x, c)))
    return pairs


def swap(value):
    return lax.ppermute(value, "chan", SWAP)


def zshift(value, step):
    return lax.ppermute(value, "head", [(i, (i + step) % NZ) for i in range(NZ)])


def dot_nt(a, b):
    return lax.dot_general(a, b, (((1,), (1,)), ((), ())), preferred_element_type=F32)


def dot_nn(a, b):
    return lax.dot_general(a, b, (((1,), (0,)), ((), ())), preferred_element_type=F32)


def dot_tn(a, b):
    return lax.dot_general(a, b, (((0,), (0,)), ((), ())), preferred_element_type=F32)


def inv_norm(u):
    return lax.rsqrt(jnp.mean(u * u, axis=-1, keepdims=True) + 1e-06)


def norm_back(u, r, dy):
    return r * dy - u * (r * r * r * jnp.mean(dy * u, axis=-1, keepdims=True))


def same_patch(rows, cols):
    ri = lax.broadcasted_iota(jnp.int32, (rows, cols), 0) % PAT
    ci = lax.broadcasted_iota(jnp.int32, (rows, cols), 1) % PAT
    return ri == ci


def softmax_rows(scores, mask):
    e = jnp.where(mask, jnp.exp(scores), 0.0)
    return e / jnp.sum(e, axis=-1, keepdims=True)


def place():
    chan = lax.axis_index("chan")
    return chan // 8, (chan // 2) % 4, chan % 2, lax.axis_index("head")


def slot_of(off):
    return jnp.where(off == 3, 1, jnp.where(off == 1, 2, jnp.where(off == 2, 3, 0)))


def off_of(slot):
    return jnp.where(slot == 1, 3, jnp.where(slot == 2, 1, jnp.where(slot == 3, 2, 0)))


def within(proj, rows, h, mask):
    q = proj[rows, pl.ds(h * 128, 128)]
    k = proj[rows, pl.ds(256 + h * 128, 128)]
    v = proj[rows, pl.ds(512 + h * 128, 128)]
    qf = q.astype(F32)
    kf = k.astype(F32)
    rq = inv_norm(qf)
    rk = inv_norm(kf)
    kn = (kf * rk).astype(BF)
    w = softmax_rows(dot_nt(q, kn) * (rq * FAC), mask)
    return qf, kf, v, rq, rk, kn, w


def prepare_kernel(tokens, position, gain, message):
    hidden = tokens[...].astype(F32) + position[...].astype(F32)[:, None, :]
    message[0:128, :] = hidden.reshape(128, 1024).astype(BF)
    message[128:136, :] = jnp.broadcast_to(gain[...], (8, 1024))


def norm_kernel(p0, p1, p2, p3, normed, inv):
    parts = (p0, p1, p2, p3)
    square = jnp.zeros((128, 1), F32)
    for p in parts:
        h = p[0:128, :].astype(F32)
        square = square + jnp.sum(h * h, axis=-1, keepdims=True)
    r = lax.rsqrt(square * (1.0 / 4096) + 1e-05)
    inv[...] = jnp.broadcast_to(r, (128, 128))
    for n, p in enumerate(parts):
        for b in range(4):
            cols = pl.ds(b * 256, 256)
            h = p[0:128, cols].astype(F32)
            g = p[128:136, cols].astype(F32)[0:1]
            normed[n * 4 + b] = (h * r * g).astype(BF)


PIECES = (
    (0, 1), (1, 2), (3, 1), (4, 1), (8, 1), (5, 2), (9, 2), (7, 1), (11, 1),
    (12, "a"), (12, "b"), (13, 1), (14, 1), (15, "a"), (15, "b"),
)


def project_kernel(own, oth, *refs):
    pieces = refs[:15]
    proj, agg, wall, wv, acc, sems, out_sems = refs[15:]
    copies = []
    for n, (ref, (slot, size)) in enumerate(zip(pieces, PIECES)):
        if size == "a":
            dst = wv.at[slot, 0:1]
        elif size == "b":
            dst = wv.at[slot, 1:2]
        else:
            dst = wv.at[slot:slot + size]
        copy = pltpu.make_async_copy(ref, dst, sems.at[n])
        copy.start()
        copies.append(copy)
    y, x, core, z = place()
    lead = core == 0
    acc[...] = jnp.zeros_like(acc)

    def step(i, carry):
        s3 = off_of(i // 4)
        s1 = off_of(i % 4)
        by = (y + jnp.where(lead, s3, s1)) % 4
        bx = (x + jnp.where(lead, s1, s3)) % 4
        blk = ((z + 4 - by) % 4) * 4 + bx
        lhs = jnp.concatenate([own[blk], oth[blk]], 0)
        for j in range(3):
            w = wv[i, :, j].reshape(256, 256)
            acc[:, j * 256:(j + 1) * 256] += dot_nn(lhs, w)
        return carry

    for copy in copies[:9]:
        copy.wait()
    lax.fori_loop(0, 12, step, 0)
    for copy in copies[9:]:
        copy.wait()
    back = pltpu.make_async_copy(wv, wall, out_sems.at[0])
    back.start()
    lax.fori_loop(12, 16, step, 0)
    proj[...] = acc[...].astype(BF)
    mask = same_patch(128, 128)
    for g in range(2):
        for h in range(2):
            _, _, v, _, _, _, w = within(proj, pl.ds(g * 128, 128), h, mask)
            f = dot_nn(w.astype(BF), v)
            m = jnp.sum(f.reshape(CHG, PAT, HD), axis=0) * (1.0 / CHG)
            agg[:, h, pl.ds(g * PAT, PAT), :] = jnp.broadcast_to(m.astype(BF)[None], (16, PAT, HD))
    back.wait()


def across_kernel(proj, agg, gm, mix_own, mix_oth, gg, gagg):
    mask = same_patch(256, 256)
    small = same_patch(128, 128)
    for h in range(2):
        cols = pl.ds(h * 128, 128)
        q = proj[:, cols]
        qf = q.astype(F32)
        rq = inv_norm(qf)
        a = agg[:, h].reshape(256, HD)
        af = a.astype(F32)
        ra = inv_norm(af)
        an = (af * ra).astype(BF)
        s = dot_nt(q, an) * (rq * FAC)
        w = softmax_rows(s, mask)
        wb = w.astype(BF)
        second = dot_nn(wb, a)
        for g, ref in enumerate((mix_own, mix_oth)):
            fine = within(proj, pl.ds(g * 128, 128), h, small)
            first = dot_nn(fine[6].astype(BF), fine[2])
            ref[:, cols] = (first + second[g * 128:(g + 1) * 128]).astype(BF)
        gf = gm[:, cols]
        g = gf.astype(BF)
        dw = dot_nt(g, a)
        ds = w * (dw - jnp.sum(w * dw, axis=-1, keepdims=True)) * FAC
        dsb = ds.astype(BF)
        gg[:, cols] = gf
        gg[:, pl.ds(256 + h * 128, 128)] = norm_back(qf, rq, dot_nn(dsb, an))
        dan = dot_tn(dsb, (qf * rq).astype(BF))
        da = dot_tn(wb, g) + norm_back(af, ra, dan)
        gagg[:, h] = da.astype(BF).reshape(16, 16, HD)


def quarter_slots(d):
    y, x, core, z = place()
    by = (z + d) % 4
    py = slot_of((by + 4 - y) % 4)
    slots = []
    for bx in range(4):
        px = slot_of((bx + 4 - x) % 4)
        slots.append(jnp.where(core == 0, py * 4 + px, px * 4 + py))
    return slots


def fetch(wall, wv, sems, d, at):
    copies = []
    for bx, slot in enumerate(quarter_slots(d)):
        copy = pltpu.make_async_copy(wall.at[slot], wv.at[at + bx], sems.at[at + bx])
        copy.start()
        copies.append(copy)
    return copies


def block_product(stk, wv, n):
    r = jnp.zeros((256, 256), F32)
    for j in range(3):
        r = r + dot_nt(stk[:, j * 256:(j + 1) * 256], wv[n, :, j].reshape(256, 256))
    return r


def back_kernel(proj, gg, ragg, wall, own, oth, stk, corr_own, corr_oth, wv, sems):
    copies = fetch(wall, wv, sems, 2, 0)
    own_grad = jnp.sum(ragg[...].astype(F32), axis=0) * (1.0 / CHG)
    mask = same_patch(128, 128)
    for g, ref in enumerate((corr_own, corr_oth)):
        rows = pl.ds(g * 128, 128)
        total = jnp.zeros((128, 1), F32)
        for h in range(2):
            cols = pl.ds(h * 128, 128)
            qf, kf, v, rq, rk, kn, w = within(proj, rows, h, mask)
            og = own_grad[h, g * PAT:(g + 1) * PAT, :]
            gf = gg[rows, cols] + jnp.broadcast_to(og[None], (CHG, PAT, HD)).reshape(128, HD)
            gb = gf.astype(BF)
            dv = dot_tn(w.astype(BF), gb)
            dw = dot_nt(gb, v)
            ds = w * (dw - jnp.sum(w * dw, axis=-1, keepdims=True)) * FAC
            dsb = ds.astype(BF)
            dq = norm_back(qf, rq, dot_nn(dsb, kn)) + gg[rows, pl.ds(256 + h * 128, 128)]
            dk = norm_back(kf, rk, dot_tn(dsb, (qf * rq).astype(BF)))
            dq = dq.astype(BF)
            dk = dk.astype(BF)
            dv = dv.astype(BF)
            stk[rows, cols] = dq
            stk[rows, pl.ds(256 + h * 128, 128)] = dk
            stk[rows, pl.ds(512 + h * 128, 128)] = dv
            prod = dq.astype(F32) * qf + dk.astype(F32) * kf + dv.astype(F32) * v.astype(F32)
            total = total + jnp.sum(prod, axis=-1, keepdims=True)
        ref[...] = jnp.broadcast_to(total, (128, 128))
    for copy in copies:
        copy.wait()

    def step(bx, carry):
        r = block_product(stk, wv, bx)
        cols = pl.ds(pl.multiple_of(bx * 256, 256), 256)
        own[:, cols] = r[0:128].astype(BF)
        oth[:, cols] = r[128:256].astype(BF)
        return carry

    lax.fori_loop(0, 4, step, 0)


def rest_kernel(stk, wall, own, oth, wv, sems):
    copies = []
    for n, d in enumerate((1, 3, 0)):
        copies.append(fetch(wall, wv, sems, d, n * 4))
    for n in range(3):
        for copy in copies[n]:
            copy.wait()

        def step(bx, carry):
            r = block_product(stk, wv, n * 4 + bx)
            cols = pl.ds(pl.multiple_of(bx * 256, 256), 256)
            own[n, :, cols] = r[0:128].astype(BF)
            oth[n, :, cols] = r[128:256].astype(BF)
            return carry

        lax.fori_loop(0, 4, step, 0)


def combine(mine, got, part, inv, corr_own, corr_got):
    r = inv[:, 0:1]
    c = (corr_own[:, 0:1] + corr_got[:, 0:1]) * (r * (1.0 / 4096))
    h = part[0:128, :].astype(F32)
    g = part[128:136, :].astype(F32)[0:1]
    return r * (g * (mine.astype(F32) + got.astype(F32)) - h * c)


def one_kernel(mine, got, part, inv, corr_own, corr_got, out):
    out[...] = combine(mine[...], got[...], part, inv, corr_own, corr_got).astype(BF)


def two_kernel(mine, got, part_a, part_b, inv, corr_own, corr_got, out_a, out_b):
    out_a[...] = combine(mine[0], got[0], part_a, inv, corr_own, corr_got).astype(BF)
    out_b[...] = combine(mine[1], got[1], part_b, inv, corr_own, corr_got).astype(BF)


def last_kernel(mine, got, part, inv, corr_own, corr_got, cot, r1, r2, r3, out):
    grad = combine(mine[2], got[2], part, inv, corr_own, corr_got)
    grad = grad + r1[...].astype(F32) + r2[...].astype(F32) + r3[...].astype(F32)
    out[...] = (cot[...].astype(F32) + grad).astype(BF)


VM = pl.BlockSpec(memory_space=pltpu.VMEM)
AN = pl.BlockSpec(memory_space=pl.ANY)
HB = pl.BlockSpec(memory_space=pltpu.HBM)
PARAMS = pltpu.CompilerParams(vmem_limit_bytes=16 * 1024 * 1024)


def shape(dims, dtype):
    return jax.ShapeDtypeStruct(dims, dtype)


def call(kernel, ins, outs, args, scratch=()):
    return pl.pallas_call(
        kernel,
        in_specs=ins,
        out_specs=[spec for spec, _ in outs],
        out_shape=[sh for _, sh in outs],
        scratch_shapes=list(scratch),
        compiler_params=PARAMS,
    )(*args)


BLOCK = (2, 3, 128, 256)


def prepare(tokens, position, gain):
    return call(prepare_kernel, [VM] * 3, [(VM, shape((136, 1024), BF))], (tokens, position, gain))[0]


def normalise(parts):
    return call(
        norm_kernel, [VM] * 4,
        [(VM, shape((16, 128, 256), BF)), (VM, shape((128, 128), F32))], parts,
    )


def project(own, oth, weights):
    return call(
        project_kernel, [VM, VM] + [AN] * 15,
        [(VM, shape((256, 768), BF)), (VM, shape((16, 2, 16, HD), BF)), (HB, shape((16,) + BLOCK, BF))],
        (own, oth) + weights,
        (
            pltpu.VMEM((16,) + BLOCK, BF), pltpu.VMEM((256, 768), F32),
            pltpu.SemaphoreType.DMA((15,)), pltpu.SemaphoreType.DMA((1,)),
        ),
    )


def across(proj, agg, gm):
    return call(
        across_kernel, [VM] * 3,
        [
            (VM, shape((128, 256), BF)), (VM, shape((128, 256), BF)),
            (VM, shape((256, 512), F32)), (VM, shape((16, 2, 16, HD), BF)),
        ],
        (proj, agg, gm),
    )


def backward(proj, gg, ragg, wall):
    return call(
        back_kernel, [VM] * 3 + [HB],
        [
            (VM, shape((128, 1024), BF)), (VM, shape((128, 1024), BF)), (VM, shape((256, 768), BF)),
            (VM, shape((128, 128), F32)), (VM, shape((128, 128), F32)),
        ],
        (proj, gg, ragg, wall),
        (pltpu.VMEM((4,) + BLOCK, BF), pltpu.SemaphoreType.DMA((4,))),
    )


def rest(stk, wall):
    return call(
        rest_kernel, [VM, HB],
        [(VM, shape((3, 128, 1024), BF)), (VM, shape((3, 128, 1024), BF))],
        (stk, wall),
        (pltpu.VMEM((12,) + BLOCK, BF), pltpu.SemaphoreType.DMA((12,))),
    )


def own_weights(qkv_weight, core):
    mine = lax.dynamic_slice_in_dim(qkv_weight, core * 256, 256, 2)
    other = lax.dynamic_slice_in_dim(qkv_weight, (1 - core) * 256, 256, 2)
    got = swap(other)
    lead = core == 0
    return jnp.stack([jnp.where(lead, mine, got), jnp.where(lead, got, mine)])


def gather_weights(own):
    def near(value, step):
        return lax.ppermute(value, "chan", ring(True, step))

    def cross(value, step):
        return lax.ppermute(value, "chan", ring(False, step))

    r = near(own, 1)
    l = near(own, -1)
    up = cross(own, 1)
    down = cross(own, -1)
    pair = jnp.stack([r, l])

    far = jnp.concatenate([near(r[:1], 1), near(l[1:], -1)], 0)
    pair_up = cross(pair, 1)
    pair_down = cross(pair, -1)
    over_a = cross(up[:1], 1)
    over_b = cross(down[1:], -1)
    far_up = cross(far, 1)
    far_down = cross(far, -1)
    pair_a = cross(pair_up[0], 1)
    pair_b = cross(pair_down[1], -1)
    far_a = cross(far_up[:1], 1)
    far_b = cross(far_down[1:], -1)

    def whole(value):
        return value.reshape((-1,) + value.shape[-4:])

    lead = tuple(whole(v) for v in (own, pair, far, up, down, pair_up, pair_down, far_up, far_down))
    tail = (over_a, over_b, whole(pair_a), whole(pair_b), far_a, far_b)
    return lead + tail, far


def layer(tokens, position, gain, qkv_weight, out_weight, cotangent):
    _, _, core, z = place()
    lead = core == 0

    own_w = own_weights(qkv_weight, core)
    message = prepare(tokens, position, gain.reshape(1, 1024))
    h_parts = [message] + [zshift(message, d) for d in (1, 2, 3)]
    weights, far = gather_weights(own_w)

    waited, _ = lax.optimization_barrier((h_parts, far))
    normed, inv_rms = normalise(waited)
    cot = cotangent.reshape(128, 1024)
    cot_b, normed = lax.optimization_barrier((cot, normed))
    c_parts = [cot_b] + [zshift(cot_b, d) for d in (1, 2, 3)]
    normed_other = swap(normed)
    proj, agg, wall = project(normed, normed_other, weights)
    agg_all = lax.all_to_all(agg, "chan", 0, 0, axis_index_groups=SAME_CORE, tiled=True)

    gm_all = sum(
        dot_nt(c, lax.dynamic_slice_in_dim(out_weight, ((z + 4 - d) % 4) * 1024, 1024, 1))
        for d, c in enumerate(c_parts)
    )
    gm_mine = jnp.where(lead, gm_all[:, :256], gm_all[:, 256:])
    gm_other = jnp.where(lead, gm_all[:, 256:], gm_all[:, :256])
    gm = jnp.concatenate([gm_mine, swap(gm_other)], 0)

    mix_own, mix_oth, gg, gagg = across(proj, agg_all, gm)
    ragg = lax.all_to_all(gagg, "chan", 0, 0, axis_index_groups=SAME_CORE, tiled=True)

    mix_got = swap(mix_oth)
    mix = jnp.concatenate([jnp.where(lead, mix_own, mix_got), jnp.where(lead, mix_got, mix_own)], 1)
    part = dot_nn(mix, out_weight)

    def quarter(value, d):
        return lax.dynamic_slice_in_dim(value, ((z + d) % 4) * 1024, 1024, 1)

    part_b = part.astype(BF)
    summed = quarter(part, 0)
    for d in (1, 2, 3):
        summed = summed + zshift(quarter(part_b, d), d).astype(F32)
    layer_out = (summed + message[:128].astype(F32)).astype(BF)

    own2, oth2, stk, corr_own, corr_oth = backward(proj, gg, ragg, wall)
    got2 = swap(oth2)
    corr_got = swap(corr_oth)
    own_r, oth_r = rest(stk, wall)
    got_r = swap(oth_r)
    scal = (inv_rms, corr_own, corr_got)
    msg2, = call(one_kernel, [VM] * 6, [(VM, shape((128, 1024), BF))], (own2, got2, h_parts[2]) + scal)
    r2 = zshift(msg2, 2)
    msg1, msg3 = call(
        two_kernel, [VM] * 7, [(VM, shape((128, 1024), BF))] * 2,
        (own_r, got_r, h_parts[3], h_parts[1]) + scal,
    )
    r1 = zshift(msg1, 1)
    r3 = zshift(msg3, 3)
    input_grad, = call(
        last_kernel, [VM] * 10, [(VM, shape((128, 1024), BF))],
        (own_r, got_r, h_parts[0]) + scal + (cot, r1, r2, r3),
    )
    return layer_out.reshape(16, 8, 1024), input_grad.reshape(16, 8, 1024)


def solution(mesh):
    return jax.shard_map(
        layer,
        mesh=mesh,
        in_specs=(
            P("chan", "region", "head"),
            P("chan", "head"),
            P("head"),
            P(None, "chan", "head"),
            P("head", None),
            P("chan", "region", "head"),
        ),
        out_specs=(P("chan", "region", "head"), P("chan", "region", "head")),
        check_vma=False,
    )
```

profile of v0, /device:TPU:64, one launch (start us, length us, event | category | flops | bytes accessed | tf_op | source)
XLA Modules:
  0.0 191.4 jit_solution(5195595037818266879)
XLA Ops:
  25.6 3.3 %collective-permute-done.7 = bf16[1,3,128,256]{3,2,1,0:T(8,128)(2,1)S(1)} collective-permute-done((bf16[1,3,128,256]{3,2,1,0:T(8,128)(2,1)S(1)}, bf16[1,3,128,256]{3,2,1,0:T(8,128)(2,1)S(1)}, u32[]{:S(2)}, u32[]{:S(2)}) %collective-permute-start.7) | collective-permute-done | bytes 196640 | tf_op jit(solution)/shard_map/ppermute | solution.py:409
  31.2 5.5 %collective-permute-done.2.p3.part_a = bf16[136,1024]{1,0:T(8,128)(2,1)S(1)} collective-permute-done((bf16[136,1024]{1,0:T(8,128)(2,1)S(1)}, bf16[136,1024]{1,0:T(8,128)(2,1)S(1)}, u32[]{:S(2)}, u32[]{:S(2)}) %collective-permute-start.2) | collective-permute-done | bytes 278560 | tf_op jit(solution)/shard_map/ppermute | solution.py:42
  38.2 2.5 %collective-permute-start.23 = (bf16[128,1024]{1,0:T(8,128)(2,1)S(1)}, bf16[128,1024]{1,0:T(8,128)(2,1)}, u32[]{:S(2)}, u32[]{:S(2)}) collective-permute-start(bf16[128,1024]{1,0:T(8,128)(2,1)S(1)} %bitcast.28), channel_id=1, source_target_pairs={{0,6},{2,0},{4,2},{6,4},{1,7},{3,1},{5,3},{7,5},{8,14},{10,8},{12,... | collective-permute-start | bytes 786440 | tf_op jit(solution)/shard_map/ppermute | solution.py:42
  47.8 3.0 %collective-permute-start.14 = (bf16[2,3,128,256]{3,2,1,0:T(8,128)(2,1)}, bf16[2,3,128,256]{3,2,1,0:T(8,128)(2,1)S(1)}, u32[]{:S(2)}, u32[]{:S(2)}) collective-permute-start(bf16[2,3,128,256]{3,2,1,0:T(8,128)(2,1)} %constant_dynamic-update-slice_fusion), channel_id=1, source_target_pairs={{0,192},{8,56},{16,208},{24,8},{32,224},{40,24},{48,240},{56,40},{... | collective-permute-start | bytes 1179656 | tf_op jit(solution)/shard_map/ppermute | solution.py:412
  60.0 6.7 %collective-permute-done.22 = bf16[128,1024]{1,0:T(8,128)(2,1)S(1)} collective-permute-done((bf16[128,1024]{1,0:T(8,128)(2,1)S(1)}, bf16[128,1024]{1,0:T(8,128)(2,1)S(1)}, u32[]{:S(2)}, u32[]{:S(2)}) %collective-permute-start.22) | collective-permute-done | bytes 262176 | tf_op jit(solution)/shard_map/ppermute | solution.py:42
  66.7 2.9 %collective-permute-start.16 = (bf16[1,3,128,256]{3,2,1,0:T(8,128)(2,1)S(1)}, bf16[1,3,128,256]{3,2,1,0:T(8,128)(2,1)S(1)}, u32[]{:S(2)}, u32[]{:S(2)}) collective-permute-start(bf16[1,3,128,256]{3,2,1,0:T(8,128)(2,1)S(1)} %slice.49), channel_id=1, source_target_pairs={{0,192},{8,56},{16,208},{24,8},{32,224},{40,24},{48,240},{56,40},{... | collective-permute-start | bytes 589832 | tf_op jit(solution)/shard_map/ppermute | solution.py:412
  69.5 3.2 %collective-permute-start.18 = (bf16[2,3,128,256]{3,2,1,0:T(8,128)(2,1)S(1)}, bf16[2,3,128,256]{3,2,1,0:T(8,128)(2,1)S(1)}, u32[]{:S(2)}, u32[]{:S(2)}) collective-permute-start(bf16[2,3,128,256]{3,2,1,0:T(8,128)(2,1)S(1)} %slice_bitcast_fusion), channel_id=1, source_target_pairs={{0,192},{8,56},{16,208},{24,8},{32,224},{40,24},{48,240},{56,40},{... | collective-permute-start | bytes 1179656 | tf_op jit(solution)/shard_map/ppermute | solution.py:412
  74.7 3.2 %collective-permute-start.20 = (bf16[1,3,128,256]{3,2,1,0:T(8,128)(2,1)S(1)}, bf16[1,3,128,256]{3,2,1,0:T(8,128)(2,1)S(1)}, u32[]{:S(2)}, u32[]{:S(2)}) collective-permute-start(bf16[1,3,128,256]{3,2,1,0:T(8,128)(2,1)S(1)} %slice.53), channel_id=1, source_target_pairs={{0,192},{8,56},{16,208},{24,8},{32,224},{40,24},{48,240},{56,40},{... | collective-permute-start | bytes 589832 | tf_op jit(solution)/shard_map/ppermute | solution.py:412
  78.6 2.9 %collective-permute-done.19.refs_13_ = bf16[1,3,128,256]{3,2,1,0:T(8,128)(2,1)S(1)} collective-permute-done((bf16[1,3,128,256]{3,2,1,0:T(8,128)(2,1)S(1)}, bf16[1,3,128,256]{3,2,1,0:T(8,128)(2,1)S(1)}, u32[]{:S(2)}, u32[]{:S(2)}) %collective-permute-start.19) | collective-permute-done | bytes 196640 | tf_op jit(solution)/shard_map/ppermute | solution.py:412
  81.5 8.3 %shard_map.79 = (bf16[256,768]{1,0:T(8,128)(2,1)S(1)}, bf16[16,2,16,128]{3,2,1,0:T(8,128)(2,1)S(1)}, bf16[16,2,3,128,256]{4,3,2,1,0:T(8,128)(2,1)S(1)}) custom-call(bf16[16,128,256]{2,1,0:T(8,128)(2,1)S(1)} %copy-done.6, bf16[16,128,256]{2,1,0:T(8,128)(2,1)S(1)} %collective-permute-done.8.oth, bf16[1,2,3,128,256]{4,3,2,1,0:T(8,128)(2,1)S(1)} %get-tuple-element.55.refs_0_, ...), custom_call_target="tpu_custom_call" | custom-call | tf_op jit(solution)/shard_map/pallas_call | solution.py:331
  89.9 2.7 %copy-done = bf16[16,2,3,128,256]{4,3,2,1,0:T(8,128)(2,1)} copy-done((bf16[16,2,3,128,256]{4,3,2,1,0:T(8,128)(2,1)}, bf16[16,2,3,128,256]{4,3,2,1,0:T(8,128)(2,1)S(1)}, u32[]{:S(2)}) %copy-start) | copy-done | bytes 6291480
  93.2 6.1 %all-to-all-start = ((bf16[16,2,16,128]{3,2,1,0:T(8,128)(2,1)}), bf16[16,2,16,128]{3,2,1,0:T(8,128)(2,1)S(1)}, u32[]{:S(2)}, u32[]{:S(2)}) async-start(bf16[16,2,16,128]{3,2,1,0:T(8,128)(2,1)} %copy-done.8), calls=%async_computation | async-start | bytes 262144 | tf_op jit(solution)/shard_map/all_to_all | solution.py:456
  100.3 7.0 %all-to-all-done.agg = bf16[16,2,16,128]{3,2,1,0:T(8,128)(2,1)S(1)} async-done(((bf16[16,2,16,128]{3,2,1,0:T(8,128)(2,1)}), bf16[16,2,16,128]{3,2,1,0:T(8,128)(2,1)S(1)}, u32[]{:S(2)}, u32[]{:S(2)}) %all-to-all-start) | async-done | bytes 131104 | tf_op jit(solution)/shard_map/all_to_all | solution.py:456
  107.2 2.7 %shard_map.80 = (bf16[128,256]{1,0:T(8,128)(2,1)S(1)}, bf16[128,256]{1,0:T(8,128)(2,1)S(1)}, f32[256,512]{1,0:T(8,128)S(1)}, bf16[16,2,16,128]{3,2,1,0:T(8,128)(2,1)}) custom-call(bf16[256,768]{1,0:T(8,128)(2,1)S(1)} %get-tuple-element.32.proj, bf16[16,2,16,128]{3,2,1,0:T(8,128)(2,1)S(1)} %all-to-all-done.agg, f32[256,256]{1,0:T(8,128)S(1)} %pad_maximum_fusion.2.gm), custom_call_target="tpu_custom_call" | custom-call | tf_op jit(solution)/shard_map/pallas_call | solution.py:331
  110.0 3.7 %all-to-all-start.1 = ((bf16[16,2,16,128]{3,2,1,0:T(8,128)(2,1)}), bf16[16,2,16,128]{3,2,1,0:T(8,128)(2,1)S(1)}, u32[]{:S(2)}, u32[]{:S(2)}) async-start(bf16[16,2,16,128]{3,2,1,0:T(8,128)(2,1)} %get-tuple-element.38), calls=%async_computation.1 | async-start | bytes 262144 | tf_op jit(solution)/shard_map/all_to_all | solution.py:467
  113.8 8.2 %all-to-all-done.1.ragg = bf16[16,2,16,128]{3,2,1,0:T(8,128)(2,1)S(1)} async-done(((bf16[16,2,16,128]{3,2,1,0:T(8,128)(2,1)}), bf16[16,2,16,128]{3,2,1,0:T(8,128)(2,1)S(1)}, u32[]{:S(2)}, u32[]{:S(2)}) %all-to-all-start.1) | async-done | bytes 131104 | tf_op jit(solution)/shard_map/all_to_all | solution.py:467
  121.9 2.8 %copy-done.1 = bf16[16,2,3,128,256]{4,3,2,1,0:T(8,128)(2,1)S(1)} copy-done((bf16[16,2,3,128,256]{4,3,2,1,0:T(8,128)(2,1)S(1)}, bf16[16,2,3,128,256]{4,3,2,1,0:T(8,128)(2,1)}, u32[]{:S(2)}) %copy-start.1) | copy-done | bytes 6291480
  124.7 4.2 %shard_map.81 = (bf16[128,1024]{1,0:T(8,128)(2,1)S(1)}, bf16[128,1024]{1,0:T(8,128)(2,1)S(1)}, bf16[256,768]{1,0:T(8,128)(2,1)S(1)}, f32[128,128]{1,0:T(8,128)S(1)}, f32[128,128]{1,0:T(8,128)S(1)}) custom-call(bf16[256,768]{1,0:T(8,128)(2,1)S(1)} %get-tuple-element.32.proj, f32[256,512]{1,0:T(8,128)S(1)} %get-tuple-element.37.gg, ...), custom_call_target="tpu_custom_call" | custom-call | tf_op jit(solution)/shard_map/pallas_call | solution.py:331
  129.0 6.1 %shard_map.82 = (bf16[3,128,1024]{2,1,0:T(8,128)(2,1)S(1)}, bf16[3,128,1024]{2,1,0:T(8,128)(2,1)S(1)}) custom-call(bf16[256,768]{1,0:T(8,128)(2,1)S(1)} %get-tuple-element.40.stk, bf16[16,2,3,128,256]{4,3,2,1,0:T(8,128)(2,1)S(1)} %copy-done.2), custom_call_target="tpu_custom_call" | custom-call | tf_op jit(solution)/shard_map/pallas_call | solution.py:331
  140.6 4.3 %collective-permute-start.27 = (bf16[128,1024]{1,0:T(8,128)(2,1)}, bf16[128,1024]{1,0:T(8,128)(2,1)}, u32[]{:S(2)}, u32[]{:S(2)}) collective-permute-start(bf16[128,1024]{1,0:T(8,128)(2,1)} %get-tuple-element.52), channel_id=1, source_target_pairs={{0,4},{2,6},{4,0},{6,2},{1,5},{3,7},{5,1},{7,3},{8,12},{10,14},{12... | collective-permute-start | bytes 786440 | tf_op jit(solution)/shard_map/ppermute | solution.py:42
  146.8 2.9 %collective-permute-start.31 = (bf16[128,1024]{1,0:T(8,128)(2,1)}, bf16[128,1024]{1,0:T(8,128)(2,1)S(1)}, u32[]{:S(2)}, u32[]{:S(2)}) collective-permute-start(bf16[128,1024]{1,0:T(8,128)(2,1)} %get-tuple-element.46), channel_id=1, source_target_pairs={{0,2},{2,4},{4,6},{6,0},{1,3},{3,5},{5,7},{7,1},{8,10},{10,12},{12... | collective-permute-start | bytes 786440 | tf_op jit(solution)/shard_map/ppermute | solution.py:42
  151.2 24.4 %collective-permute-done.27 = bf16[128,1024]{1,0:T(8,128)(2,1)} collective-permute-done((bf16[128,1024]{1,0:T(8,128)(2,1)}, bf16[128,1024]{1,0:T(8,128)(2,1)}, u32[]{:S(2)}, u32[]{:S(2)}) %collective-permute-start.27) | collective-permute-done | bytes 262176 | tf_op jit(solution)/shard_map/ppermute | solution.py:42
  177.8 3.3 %collective-permute-done.33.r2 = bf16[128,1024]{1,0:T(8,128)(2,1)S(1)} collective-permute-done((bf16[128,1024]{1,0:T(8,128)(2,1)S(1)}, bf16[128,1024]{1,0:T(8,128)(2,1)S(1)}, u32[]{:S(2)}, u32[]{:S(2)}) %collective-permute-start.33) | collective-permute-done | bytes 262176 | tf_op jit(solution)/shard_map/ppermute | solution.py:42
  181.1 9.2 %collective-permute-done.31.r1 = bf16[128,1024]{1,0:T(8,128)(2,1)S(1)} collective-permute-done((bf16[128,1024]{1,0:T(8,128)(2,1)}, bf16[128,1024]{1,0:T(8,128)(2,1)S(1)}, u32[]{:S(2)}, u32[]{:S(2)}) %collective-permute-start.31) | collective-permute-done | bytes 262176 | tf_op jit(solution)/shard_map/ppermute | solution.py:42
  (108 shorter events, 61.2 us)
Async XLA Ops:
  6.5 11.3 %collective-permute-start.6 = (bf16[2,3,128,256]{3,2,1,0:T(8,128)(2,1)}, bf16[2,3,128,256]{3,2,1,0:T(8,128)(2,1)S(1)}, u32[]{:S(2)}, u32[]{:S(2)}) collective-permute-start(bf16[2,3,128,256]{3,2,1,0:T(8,128)(2,1)} %get-tuple-element.56), channel_id=1, source_target_pairs={{0,48},{8,200},{16,0},{24,216},{32,16},{40,232},{48,32},{56,248},{... | collective-permute-start | bytes 1179656 | tf_op jit(solution)/shard_map/ppermute | solution.py:409
  14.6 28.1 %collective-permute-start.9 = (bf16[2,3,128,256]{3,2,1,0:T(8,128)(2,1)}, bf16[2,3,128,256]{3,2,1,0:T(8,128)(2,1)}, u32[]{:S(2)}, u32[]{:S(2)}) collective-permute-start(bf16[2,3,128,256]{3,2,1,0:T(8,128)(2,1)} %get-tuple-element.56), channel_id=1, source_target_pairs={{0,64},{8,24},{16,80},{24,40},{32,96},{40,56},{48,112},{56,8},{64,... | collective-permute-start | bytes 1179656 | tf_op jit(solution)/shard_map/ppermute | solution.py:412
  16.1 27.5 %collective-permute-start.10 = (bf16[2,3,128,256]{3,2,1,0:T(8,128)(2,1)}, bf16[2,3,128,256]{3,2,1,0:T(8,128)(2,1)}, u32[]{:S(2)}, u32[]{:S(2)}) collective-permute-start(bf16[2,3,128,256]{3,2,1,0:T(8,128)(2,1)} %get-tuple-element.56), channel_id=1, source_target_pairs={{0,192},{8,56},{16,208},{24,8},{32,224},{40,24},{48,240},{56,40},{... | collective-permute-start | bytes 1179656 | tf_op jit(solution)/shard_map/ppermute | solution.py:412
  17.8 13.4 %collective-permute-start.1 = (bf16[136,1024]{1,0:T(8,128)(2,1)S(1)}, bf16[136,1024]{1,0:T(8,128)(2,1)S(1)}, u32[]{:S(2)}, u32[]{:S(2)}) collective-permute-start(bf16[136,1024]{1,0:T(8,128)(2,1)S(1)} %shard_map.77.p0.part), channel_id=1, source_target_pairs={{0,4},{2,6},{4,0},{6,2},{1,5},{3,7},{5,1},{7,3},{8,12},{10,14},{12... | collective-permute-start | bytes 835592 | tf_op jit(solution)/shard_map/ppermute | solution.py:42
  19.0 17.7 %collective-permute-start.2 = (bf16[136,1024]{1,0:T(8,128)(2,1)S(1)}, bf16[136,1024]{1,0:T(8,128)(2,1)S(1)}, u32[]{:S(2)}, u32[]{:S(2)}) collective-permute-start(bf16[136,1024]{1,0:T(8,128)(2,1)S(1)} %shard_map.77.p0.part), channel_id=1, source_target_pairs={{0,6},{2,0},{4,2},{6,4},{1,7},{3,1},{5,3},{7,5},{8,14},{10,8},{12,... | collective-permute-start | bytes 835592 | tf_op jit(solution)/shard_map/ppermute | solution.py:42
  28.9 29.3 %collective-permute-start.11 = (bf16[2,2,3,128,256]{4,3,2,1,0:T(8,128)(2,1)S(1)}, bf16[2,2,3,128,256]{4,3,2,1,0:T(8,128)(2,1)S(1)}, u32[]{:S(2)}, u32[]{:S(2)}) collective-permute-start(bf16[2,2,3,128,256]{4,3,2,1,0:T(8,128)(2,1)S(1)} %pad_maximum_fusion.refs_1_), channel_id=1, source_target_pairs={{0,64},{8,24},{16,80},{24,40},{32,96},{40,56},{48,112},{56,8},{64,... | collective-permute-start | bytes 2359304 | tf_op jit(solution)/shard_map/ppermute | solution.py:412
  40.7 17.6 %collective-permute-start.12 = (bf16[2,2,3,128,256]{4,3,2,1,0:T(8,128)(2,1)S(1)}, bf16[2,2,3,128,256]{4,3,2,1,0:T(8,128)(2,1)S(1)}, u32[]{:S(2)}, u32[]{:S(2)}) collective-permute-start(bf16[2,2,3,128,256]{4,3,2,1,0:T(8,128)(2,1)S(1)} %pad_maximum_fusion.refs_1_), channel_id=1, source_target_pairs={{0,192},{8,56},{16,208},{24,8},{32,224},{40,24},{48,240},{56,40},{... | collective-permute-start | bytes 2359304 | tf_op jit(solution)/shard_map/ppermute | solution.py:412
  44.6 24.9 %collective-permute-start.13 = (bf16[2,3,128,256]{3,2,1,0:T(8,128)(2,1)}, bf16[2,3,128,256]{3,2,1,0:T(8,128)(2,1)S(1)}, u32[]{:S(2)}, u32[]{:S(2)}) collective-permute-start(bf16[2,3,128,256]{3,2,1,0:T(8,128)(2,1)} %constant_dynamic-update-slice_fusion), channel_id=1, source_target_pairs={{0,64},{8,24},{16,80},{24,40},{32,96},{40,56},{48,112},{56,8},{64,... | collective-permute-start | bytes 1179656 | tf_op jit(solution)/shard_map/ppermute | solution.py:412
  47.8 21.8 %collective-permute-start.14 = (bf16[2,3,128,256]{3,2,1,0:T(8,128)(2,1)}, bf16[2,3,128,256]{3,2,1,0:T(8,128)(2,1)S(1)}, u32[]{:S(2)}, u32[]{:S(2)}) collective-permute-start(bf16[2,3,128,256]{3,2,1,0:T(8,128)(2,1)} %constant_dynamic-update-slice_fusion), channel_id=1, source_target_pairs={{0,192},{8,56},{16,208},{24,8},{32,224},{40,24},{48,240},{56,40},{... | collective-permute-start | bytes 1179656 | tf_op jit(solution)/shard_map/ppermute | solution.py:412
  55.0 11.6 %collective-permute-start.22 = (bf16[128,1024]{1,0:T(8,128)(2,1)S(1)}, bf16[128,1024]{1,0:T(8,128)(2,1)S(1)}, u32[]{:S(2)}, u32[]{:S(2)}) collective-permute-start(bf16[128,1024]{1,0:T(8,128)(2,1)S(1)} %bitcast.31), channel_id=1, source_target_pairs={{0,4},{2,6},{4,0},{6,2},{1,5},{3,7},{5,1},{7,3},{8,12},{10,14},{12... | collective-permute-start | bytes 786440 | tf_op jit(solution)/shard_map/ppermute | solution.py:42
  58.2 23.3 %collective-permute-start.8 = (bf16[16,128,256]{2,1,0:T(8,128)(2,1)S(1)}, bf16[16,128,256]{2,1,0:T(8,128)(2,1)S(1)}, u32[]{:S(2)}, u32[]{:S(2)}) collective-permute-start(bf16[16,128,256]{2,1,0:T(8,128)(2,1)S(1)} %copy-done.6), channel_id=1, source_target_pairs={{0,8},{8,0},{16,24},{24,16},{32,40},{40,32},{48,56},{56,48},{64,72... | collective-permute-start | bytes 3145736 | tf_op jit(solution)/shard_map/ppermute | solution.py:38
  58.4 16.2 %collective-permute-start.15 = (bf16[1,3,128,256]{3,2,1,0:T(8,128)(2,1)S(1)}, bf16[1,3,128,256]{3,2,1,0:T(8,128)(2,1)S(1)}, u32[]{:S(2)}, u32[]{:S(2)}) collective-permute-start(bf16[1,3,128,256]{3,2,1,0:T(8,128)(2,1)S(1)} %slice.48), channel_id=1, source_target_pairs={{0,64},{8,24},{16,80},{24,40},{32,96},{40,56},{48,112},{56,8},{64,... | collective-permute-start | bytes 589832 | tf_op jit(solution)/shard_map/ppermute | solution.py:412
  69.5 12.0 %collective-permute-start.17 = (bf16[2,3,128,256]{3,2,1,0:T(8,128)(2,1)S(1)}, bf16[2,3,128,256]{3,2,1,0:T(8,128)(2,1)S(1)}, u32[]{:S(2)}, u32[]{:S(2)}) collective-permute-start(bf16[2,3,128,256]{3,2,1,0:T(8,128)(2,1)S(1)} %slice_bitcast_fusion.1), channel_id=1, source_target_pairs={{0,64},{8,24},{16,80},{24,40},{32,96},{40,56},{48,112},{56,8},{64,... | collective-permute-start | bytes 1179656 | tf_op jit(solution)/shard_map/ppermute | solution.py:412
  69.5 12.0 %collective-permute-start.18 = (bf16[2,3,128,256]{3,2,1,0:T(8,128)(2,1)S(1)}, bf16[2,3,128,256]{3,2,1,0:T(8,128)(2,1)S(1)}, u32[]{:S(2)}, u32[]{:S(2)}) collective-permute-start(bf16[2,3,128,256]{3,2,1,0:T(8,128)(2,1)S(1)} %slice_bitcast_fusion), channel_id=1, source_target_pairs={{0,192},{8,56},{16,208},{24,8},{32,224},{40,24},{48,240},{56,40},{... | collective-permute-start | bytes 1179656 | tf_op jit(solution)/shard_map/ppermute | solution.py:412
  81.5 17.7 %collective-permute-start.24 = (f32[128,256]{1,0:T(8,128)}, f32[128,256]{1,0:T(8,128)}, u32[]{:S(2)}, u32[]{:S(2)}) collective-permute-start(f32[128,256]{1,0:T(8,128)} %get-tuple-element.58), channel_id=1, source_target_pairs={{0,8},{8,0},{16,24},{24,16},{32,40},{40,32},{48,56},{56,48},{64,72... | collective-permute-start | bytes 393224 | tf_op jit(solution)/shard_map/ppermute | solution.py:38
  93.2 14.1 %all-to-all-start = ((bf16[16,2,16,128]{3,2,1,0:T(8,128)(2,1)}), bf16[16,2,16,128]{3,2,1,0:T(8,128)(2,1)S(1)}, u32[]{:S(2)}, u32[]{:S(2)}) async-start(bf16[16,2,16,128]{3,2,1,0:T(8,128)(2,1)} %copy-done.8), calls=%async_computation | async-start | bytes 262144 | tf_op jit(solution)/shard_map/all_to_all | solution.py:456
  110.0 11.9 %all-to-all-start.1 = ((bf16[16,2,16,128]{3,2,1,0:T(8,128)(2,1)}), bf16[16,2,16,128]{3,2,1,0:T(8,128)(2,1)S(1)}, u32[]{:S(2)}, u32[]{:S(2)}) async-start(bf16[16,2,16,128]{3,2,1,0:T(8,128)(2,1)} %get-tuple-element.38), calls=%async_computation.1 | async-start | bytes 262144 | tf_op jit(solution)/shard_map/all_to_all | solution.py:467
  135.1 10.7 %collective-permute-start.29 = (bf16[3,128,1024]{2,1,0:T(8,128)(2,1)S(1)}, bf16[3,128,1024]{2,1,0:T(8,128)(2,1)S(1)}, u32[]{:S(2)}, u32[]{:S(2)}) collective-permute-start(bf16[3,128,1024]{2,1,0:T(8,128)(2,1)S(1)} %get-tuple-element.42), channel_id=1, source_target_pairs={{0,8},{8,0},{16,24},{24,16},{32,40},{40,32},{48,56},{56,48},{64,72... | collective-permute-start | bytes 2359304 | tf_op jit(solution)/shard_map/ppermute | solution.py:38
  138.7 11.0 %collective-permute-start.28 = (bf16[128,1024]{1,0:T(8,128)(2,1)S(1)}, bf16[128,1024]{1,0:T(8,128)(2,1)S(1)}, u32[]{:S(2)}, u32[]{:S(2)}) collective-permute-start(bf16[128,1024]{1,0:T(8,128)(2,1)S(1)} %get-tuple-element.51), channel_id=1, source_target_pairs={{0,6},{2,0},{4,2},{6,4},{1,7},{3,1},{5,3},{7,5},{8,14},{10,8},{12,... | collective-permute-start | bytes 786440 | tf_op jit(solution)/shard_map/ppermute | solution.py:42
  140.6 34.9 %collective-permute-start.27 = (bf16[128,1024]{1,0:T(8,128)(2,1)}, bf16[128,1024]{1,0:T(8,128)(2,1)}, u32[]{:S(2)}, u32[]{:S(2)}) collective-permute-start(bf16[128,1024]{1,0:T(8,128)(2,1)} %get-tuple-element.52), channel_id=1, source_target_pairs={{0,4},{2,6},{4,0},{6,2},{1,5},{3,7},{5,1},{7,3},{8,12},{10,14},{12... | collective-permute-start | bytes 786440 | tf_op jit(solution)/shard_map/ppermute | solution.py:42
  144.9 30.7 %collective-permute-start.26 = (bf16[128,1024]{1,0:T(8,128)(2,1)}, bf16[128,1024]{1,0:T(8,128)(2,1)}, u32[]{:S(2)}, u32[]{:S(2)}) collective-permute-start(bf16[128,1024]{1,0:T(8,128)(2,1)} %get-tuple-element.50), channel_id=1, source_target_pairs={{0,2},{2,4},{4,6},{6,0},{1,3},{3,5},{5,7},{7,1},{8,10},{10,12},{12... | collective-permute-start | bytes 786440 | tf_op jit(solution)/shard_map/ppermute | solution.py:42
  145.1 36.0 %collective-permute-start.33 = (bf16[128,1024]{1,0:T(8,128)(2,1)S(1)}, bf16[128,1024]{1,0:T(8,128)(2,1)S(1)}, u32[]{:S(2)}, u32[]{:S(2)}) collective-permute-start(bf16[128,1024]{1,0:T(8,128)(2,1)S(1)} %shard_map.84), channel_id=1, source_target_pairs={{0,4},{2,6},{4,0},{6,2},{1,5},{3,7},{5,1},{7,3},{8,12},{10,14},{12... | collective-permute-start | bytes 786440 | tf_op jit(solution)/shard_map/ppermute | solution.py:42
  146.8 43.5 %collective-permute-start.31 = (bf16[128,1024]{1,0:T(8,128)(2,1)}, bf16[128,1024]{1,0:T(8,128)(2,1)S(1)}, u32[]{:S(2)}, u32[]{:S(2)}) collective-permute-start(bf16[128,1024]{1,0:T(8,128)(2,1)} %get-tuple-element.46), channel_id=1, source_target_pairs={{0,2},{2,4},{4,6},{6,0},{1,3},{3,5},{5,7},{7,1},{8,10},{10,12},{12... | collective-permute-start | bytes 786440 | tf_op jit(solution)/shard_map/ppermute | solution.py:42
  150.4 39.9 %collective-permute-start.34 = (bf16[128,1024]{1,0:T(8,128)(2,1)}, bf16[128,1024]{1,0:T(8,128)(2,1)S(1)}, u32[]{:S(2)}, u32[]{:S(2)}) collective-permute-start(bf16[128,1024]{1,0:T(8,128)(2,1)} %get-tuple-element.49), channel_id=1, source_target_pairs={{0,6},{2,0},{4,2},{6,4},{1,7},{3,1},{5,3},{7,5},{8,14},{10,8},{12,... | collective-permute-start | bytes 786440 | tf_op jit(solution)/shard_map/ppermute | solution.py:42
  (25 other events, 222.0 us)
where the time goes:
time: 192 us; the launch traced here: 191 us
  waiting for transfers between devices  77.8 us (41%)
  starting transfers between devices  58 us (30%)
  Pallas kernels  24.2 us (13%)
  local copies, waits for them, and re-layouts  15.4 us (8%)
  matrix products  9.02 us (5%)
  other arithmetic  5.79 us (3%)
    ppermute x12, waiting for transfers between devices, zshift(): lax.ppermute(value, 'head', [(i, (i + step) % NZ) for i in range(NZ)])  51.5 us
    pallas_call x9, Pallas kernels, call(): pl.pallas_call(kernel, in_specs=ins, out_specs=[spec for spec, _ in outs]...  24.2 us
    ppermute x12, starting transfers between devices, zshift(): lax.ppermute(value, 'head', [(i, (i + step) % NZ) for i in range(NZ)])  21.3 us
    ppermute x12, starting transfers between devices, cross(): return lax.ppermute(value, 'chan', ring(False, step))  20.9 us
    unnamed x25, local copies, waits for them, and re-layouts  10.2 us
    all_to_all x1, waiting for transfers between devices, layer(): lax.all_to_all(gagg, 'chan', 0, 0, axis_index_groups=SAME_CORE, tiled=True)  8.16 us
    all_to_all x1, waiting for transfers between devices, layer(): lax.all_to_all(agg, 'chan', 0, 0, axis_index_groups=SAME_CORE, tiled=True)  6.99 us
    dot_general x4, matrix products, dot_nt(): lax.dot_general(a, b, (((1,), (1,)), ((), ())), preferred_element_type=F32)  6.92 us
  transfers between devices with their start and end apart: 37, of which 13 were waited for; matrix products, arithmetic and copies ran while one was open for 9% of the time, Pallas kernels for 5%

commit v1 on v0

--- a/solution.py
+++ b/solution.py
@@ -317,6 +317,35 @@
     out[...] = (cot[...].astype(F32) + grad).astype(BF)
 
 
+def gm_kernel(c0, c1, c2, c3, ow, mine, other):
+    _, _, core, z = place()
+    for ref, which in ((mine, core), (other, 1 - core)):
+        rows = pl.ds(pl.multiple_of(which * 256, 256), 256)
+        total = jnp.zeros((128, 256), F32)
+        for d, c in enumerate((c0, c1, c2, c3)):
+            cols = pl.ds(pl.multiple_of(((z + 4 - d) % 4) * 1024, 1024), 1024)
+            total = total + dot_nt(c[...], ow[rows, cols])
+        ref[...] = total
+
+
+def out_quarter(mine, got, ow, d):
+    _, _, core, z = place()
+    cols = pl.ds(pl.multiple_of(((z + d) % 4) * 1024, 1024), 1024)
+    rows = pl.ds(pl.multiple_of(core * 256, 256), 256)
+    rows_got = pl.ds(pl.multiple_of((1 - core) * 256, 256), 256)
+    return dot_nn(mine[...], ow[rows, cols]) + dot_nn(got[...], ow[rows_got, cols])
+
+
+def out_first_kernel(mine, got, ow, o2):
+    o2[...] = out_quarter(mine, got, ow, 2).astype(BF)
+
+
+def out_rest_kernel(mine, got, ow, o1, o3, o0):
+    o1[...] = out_quarter(mine, got, ow, 1).astype(BF)
+    o3[...] = out_quarter(mine, got, ow, 3).astype(BF)
+    o0[...] = out_quarter(mine, got, ow, 0)
+
+
 VM = pl.BlockSpec(memory_space=pltpu.VMEM)
 AN = pl.BlockSpec(memory_space=pl.ANY)
 HB = pl.BlockSpec(memory_space=pltpu.HBM)
@@ -355,7 +384,7 @@
 def project(own, oth, weights):
     return call(
         project_kernel, [VM, VM] + [AN] * 15,
-        [(VM, shape((256, 768), BF)), (VM, shape((16, 2, 16, HD), BF)), (HB, shape((16,) + BLOCK, BF))],
+        [(VM, shape((256, 768), BF)), (VM, shape((16, 2, 16, HD), BF)), (HB, pltpu.HBM((16,) + BLOCK, BF))],
         (own, oth) + weights,
         (
             pltpu.VMEM((16,) + BLOCK, BF), pltpu.VMEM((256, 768), F32),
@@ -382,7 +411,7 @@
             (VM, shape((128, 1024), BF)), (VM, shape((128, 1024), BF)), (VM, shape((256, 768), BF)),
             (VM, shape((128, 128), F32)), (VM, shape((128, 128), F32)),
         ],
-        (proj, gg, ragg, wall),
+        (proj, gg, ragg, pltpu.with_memory_space_constraint(wall, pltpu.HBM)),
         (pltpu.VMEM((4,) + BLOCK, BF), pltpu.SemaphoreType.DMA((4,))),
     )
 
@@ -391,7 +420,7 @@
     return call(
         rest_kernel, [VM, HB],
         [(VM, shape((3, 128, 1024), BF)), (VM, shape((3, 128, 1024), BF))],
-        (stk, wall),
+        (stk, pltpu.with_memory_space_constraint(wall, pltpu.HBM)),
         (pltpu.VMEM((12,) + BLOCK, BF), pltpu.SemaphoreType.DMA((12,))),
     )
 
@@ -438,45 +467,47 @@
 
 
 def layer(tokens, position, gain, qkv_weight, out_weight, cotangent):
-    _, _, core, z = place()
-    lead = core == 0
+    _, _, core, _ = place()
 
     own_w = own_weights(qkv_weight, core)
     message = prepare(tokens, position, gain.reshape(1, 1024))
-    h_parts = [message] + [zshift(message, d) for d in (1, 2, 3)]
+    h_parts = [message]
+    for d in (1, 2, 3):
+        h_parts.append(zshift(message, d))
     weights, far = gather_weights(own_w)
 
     waited, _ = lax.optimization_barrier((h_parts, far))
     normed, inv_rms = normalise(waited)
     cot = cotangent.reshape(128, 1024)
     cot_b, normed = lax.optimization_barrier((cot, normed))
-    c_parts = [cot_b] + [zshift(cot_b, d) for d in (1, 2, 3)]
+    c_parts = [cot_b]
+    for d in (1, 2, 3):
+        c_parts.append(zshift(cot_b, d))
     normed_other = swap(normed)
     proj, agg, wall = project(normed, normed_other, weights)
     agg_all = lax.all_to_all(agg, "chan", 0, 0, axis_index_groups=SAME_CORE, tiled=True)
 
-    gm_all = sum(
-        dot_nt(c, lax.dynamic_slice_in_dim(out_weight, ((z + 4 - d) % 4) * 1024, 1024, 1))
-        for d, c in enumerate(c_parts)
-    )
-    gm_mine = jnp.where(lead, gm_all[:, :256], gm_all[:, 256:])
-    gm_other = jnp.where(lead, gm_all[:, 256:], gm_all[:, :256])
+    gm_mine, gm_other = call(
+        gm_kernel, [VM] * 5, [(VM, shape((128, 256), F32))] * 2, c_parts + [out_weight],
+    )
     gm = jnp.concatenate([gm_mine, swap(gm_other)], 0)
 
     mix_own, mix_oth, gg, gagg = across(proj, agg_all, gm)
     ragg = lax.all_to_all(gagg, "chan", 0, 0, axis_index_groups=SAME_CORE, tiled=True)
 
     mix_got = swap(mix_oth)
-    mix = jnp.concatenate([jnp.where(lead, mix_own, mix_got), jnp.where(lead, mix_got, mix_own)], 1)
-    part = dot_nn(mix, out_weight)
-
-    def quarter(value, d):
-        return lax.dynamic_slice_in_dim(value, ((z + d) % 4) * 1024, 1024, 1)
-
-    part_b = part.astype(BF)
-    summed = quarter(part, 0)
-    for d in (1, 2, 3):
-        summed = summed + zshift(quarter(part_b, d), d).astype(F32)
+    o2, = call(
+        out_first_kernel, [VM] * 3, [(VM, shape((128, 1024), BF))], (mix_own, mix_got, out_weight),
+    )
+    s2 = zshift(o2, 2)
+    o1, o3, o0 = call(
+        out_rest_kernel, [VM] * 3,
+        [(VM, shape((128, 1024), BF)), (VM, shape((128, 1024), BF)), (VM, shape((128, 1024), F32))],
+        (mix_own, mix_got, out_weight),
+    )
+    s1 = zshift(o1, 1)
+    s3 = zshift(o3, 3)
+    summed = o0 + s1.astype(F32) + s2.astype(F32) + s3.astype(F32)
     layer_out = (summed + message[:128].astype(F32)).astype(BF)
 
     own2, oth2, stk, corr_own, corr_oth = backward(proj, gg, ragg, wall)

time: 192 us -> 183 us (0.953)
  the two profiles are of different devices: /device:TPU:64 before, /device:TPU:192 now
where the time goes in v1:
time: 183 us
  waiting for transfers between devices  86.7 us (47%)
  starting transfers between devices  52.5 us (29%)
  Pallas kernels  26 us (14%)
  blocking collectives  11.1 us (6%)
  local copies, waits for them, and re-layouts  3.55 us (2%)
  other arithmetic  2.04 us (1%)
    ppermute x12, waiting for transfers between devices, zshift(): lax.ppermute(value, 'head', [(i, (i + step) % NZ) for i in range(NZ)])  62.9 us
    pallas_call x12, Pallas kernels, call(): pl.pallas_call(kernel, in_specs=ins, out_specs=[spec for spec, _ in outs]...  26 us
    ppermute x12, starting transfers between devices, zshift(): lax.ppermute(value, 'head', [(i, (i + step) % NZ) for i in range(NZ)])  23.1 us
    ppermute x12, starting transfers between devices, cross(): return lax.ppermute(value, 'chan', ring(False, step))  16.8 us
    all_to_all x1, blocking collectives, layer(): lax.all_to_all(gagg, 'chan', 0, 0, axis_index_groups=SAME_CORE, tiled=True)  11.1 us
    all_to_all x1, waiting for transfers between devices, layer(): lax.all_to_all(agg, 'chan', 0, 0, axis_index_groups=SAME_CORE, tiled=True)  7.95 us
    ppermute x12, waiting for transfers between devices, cross(): return lax.ppermute(value, 'chan', ring(False, step))  7.82 us
    all_to_all x1, starting transfers between devices, layer(): lax.all_to_all(agg, 'chan', 0, 0, axis_index_groups=SAME_CORE, tiled=True)  5.9 us
  transfers between devices with their start and end apart: 36, of which 16 were waited for; matrix products, arithmetic and copies ran while one was open for 1% of the time, Pallas kernels for 7%

profile of v1, /device:TPU:192, one launch (start us, length us, event | category | flops | bytes accessed | tf_op | source)
XLA Modules:
  0.0 182.8 jit_solution(4501744648331278624)
XLA Ops:
  15.4 3.0 %collective-permute-start.11 = (bf16[2,2,3,128,256]{4,3,2,1,0:T(8,128)(2,1)S(1)}, bf16[2,2,3,128,256]{4,3,2,1,0:T(8,128)(2,1)S(1)}, u32[]{:S(2)}, u32[]{:S(2)}) collective-permute-start(bf16[2,2,3,128,256]{4,3,2,1,0:T(8,128)(2,1)S(1)} %pad_maximum_fusion.refs_1_), channel_id=1, source_target_pairs={{0,64},{8,24},{16,80},{24,40},{32,96},{40,56},{48,112},{56,8},{64,... | collective-permute-start | bytes 2359304 | tf_op jit(solution)/shard_map/ppermute | solution.py:441
  18.8 8.4 %collective-permute-done.p1.part_b = bf16[136,1024]{1,0:T(8,128)(2,1)S(1)} collective-permute-done((bf16[136,1024]{1,0:T(8,128)(2,1)S(1)}, bf16[136,1024]{1,0:T(8,128)(2,1)S(1)}, u32[]{:S(2)}, u32[]{:S(2)}) %collective-permute-start) | collective-permute-done | bytes 278560 | tf_op jit(solution)/shard_map/ppermute | solution.py:42
  28.9 2.6 %collective-permute-done.1.p2.part = bf16[136,1024]{1,0:T(8,128)(2,1)S(1)} collective-permute-done((bf16[136,1024]{1,0:T(8,128)(2,1)S(1)}, bf16[136,1024]{1,0:T(8,128)(2,1)S(1)}, u32[]{:S(2)}, u32[]{:S(2)}) %collective-permute-start.1) | collective-permute-done | bytes 278560 | tf_op jit(solution)/shard_map/ppermute | solution.py:42
  34.9 4.1 %collective-permute-done.7 = bf16[1,3,128,256]{3,2,1,0:T(8,128)(2,1)S(1)} collective-permute-done((bf16[1,3,128,256]{3,2,1,0:T(8,128)(2,1)S(1)}, bf16[1,3,128,256]{3,2,1,0:T(8,128)(2,1)S(1)}, u32[]{:S(2)}, u32[]{:S(2)}) %collective-permute-start.7) | collective-permute-done | bytes 196640 | tf_op jit(solution)/shard_map/ppermute | solution.py:438
  39.0 3.7 %collective-permute-done.2.p3.part_a = bf16[136,1024]{1,0:T(8,128)(2,1)S(1)} collective-permute-done((bf16[136,1024]{1,0:T(8,128)(2,1)S(1)}, bf16[136,1024]{1,0:T(8,128)(2,1)S(1)}, u32[]{:S(2)}, u32[]{:S(2)}) %collective-permute-start.2) | collective-permute-done | bytes 278560 | tf_op jit(solution)/shard_map/ppermute | solution.py:42
  43.2 3.2 %collective-permute-start.21 = (bf16[128,1024]{1,0:T(8,128)(2,1)S(1)}, bf16[128,1024]{1,0:T(8,128)(2,1)S(1)}, u32[]{:S(2)}, u32[]{:S(2)}) collective-permute-start(bf16[128,1024]{1,0:T(8,128)(2,1)S(1)} %bitcast.23), channel_id=1, source_target_pairs={{0,2},{2,4},{4,6},{6,0},{1,3},{3,5},{5,7},{7,1},{8,10},{10,12},{12... | collective-permute-start | bytes 786440 | tf_op jit(solution)/shard_map/ppermute | solution.py:42
  47.3 4.9 %collective-permute-done.16.refs_10_ = bf16[1,3,128,256]{3,2,1,0:T(8,128)(2,1)S(1)} collective-permute-done((bf16[1,3,128,256]{3,2,1,0:T(8,128)(2,1)S(1)}, bf16[1,3,128,256]{3,2,1,0:T(8,128)(2,1)S(1)}, u32[]{:S(2)}, u32[]{:S(2)}) %collective-permute-start.16) | collective-permute-done | bytes 196640 | tf_op jit(solution)/shard_map/ppermute | solution.py:441
  52.6 2.9 %collective-permute-start.14 = (bf16[2,3,128,256]{3,2,1,0:T(8,128)(2,1)S(1)}, bf16[2,3,128,256]{3,2,1,0:T(8,128)(2,1)S(1)}, u32[]{:S(2)}, u32[]{:S(2)}) collective-permute-start(bf16[2,3,128,256]{3,2,1,0:T(8,128)(2,1)S(1)} %constant_dynamic-update-slice_fusion), channel_id=1, source_target_pairs={{0,192},{8,56},{16,208},{24,8},{32,224},{40,24},{48,240},{56,40},{... | collective-permute-start | bytes 1179656 | tf_op jit(solution)/shard_map/ppermute | solution.py:441
  55.9 2.8 %collective-permute-start.23 = (bf16[128,1024]{1,0:T(8,128)(2,1)S(1)}, bf16[128,1024]{1,0:T(8,128)(2,1)S(1)}, u32[]{:S(2)}, u32[]{:S(2)}) collective-permute-start(bf16[128,1024]{1,0:T(8,128)(2,1)S(1)} %bitcast.25), channel_id=1, source_target_pairs={{0,6},{2,0},{4,2},{6,4},{1,7},{3,1},{5,3},{7,5},{8,14},{10,8},{12,... | collective-permute-start | bytes 786440 | tf_op jit(solution)/shard_map/ppermute | solution.py:42
  58.8 6.7 %collective-permute-done.22.c2 = bf16[128,1024]{1,0:T(8,128)(2,1)S(1)} collective-permute-done((bf16[128,1024]{1,0:T(8,128)(2,1)S(1)}, bf16[128,1024]{1,0:T(8,128)(2,1)S(1)}, u32[]{:S(2)}, u32[]{:S(2)}) %collective-permute-start.22) | collective-permute-done | bytes 262176 | tf_op jit(solution)/shard_map/ppermute | solution.py:42
  66.0 2.7 %collective-permute-start.18 = (bf16[2,3,128,256]{3,2,1,0:T(8,128)(2,1)S(1)}, bf16[2,3,128,256]{3,2,1,0:T(8,128)(2,1)S(1)}, u32[]{:S(2)}, u32[]{:S(2)}) collective-permute-start(bf16[2,3,128,256]{3,2,1,0:T(8,128)(2,1)S(1)} %slice_bitcast_fusion), channel_id=1, source_target_pairs={{0,192},{8,56},{16,208},{24,8},{32,224},{40,24},{48,240},{56,40},{... | collective-permute-start | bytes 1179656 | tf_op jit(solution)/shard_map/ppermute | solution.py:441
  73.7 2.9 %collective-permute-done.19.refs_13_ = bf16[1,3,128,256]{3,2,1,0:T(8,128)(2,1)S(1)} collective-permute-done((bf16[1,3,128,256]{3,2,1,0:T(8,128)(2,1)S(1)}, bf16[1,3,128,256]{3,2,1,0:T(8,128)(2,1)S(1)}, u32[]{:S(2)}, u32[]{:S(2)}) %collective-permute-start.19) | collective-permute-done | bytes 196640 | tf_op jit(solution)/shard_map/ppermute | solution.py:441
  76.6 9.5 %shard_map.79 = (bf16[256,768]{1,0:T(8,128)(2,1)S(1)}, bf16[16,2,16,128]{3,2,1,0:T(8,128)(2,1)}, bf16[16,2,3,128,256]{4,3,2,1,0:T(8,128)(2,1)}) custom-call(bf16[16,128,256]{2,1,0:T(8,128)(2,1)S(1)} %get-tuple-element.36.own, bf16[16,128,256]{2,1,0:T(8,128)(2,1)S(1)} %collective-permute-done.8.oth, ...), custom_call_target="tpu_custom_call" | custom-call | tf_op jit(solution)/shard_map/pallas_call | solution.py:360
  86.1 5.9 %all-to-all-start = ((bf16[16,2,16,128]{3,2,1,0:T(8,128)(2,1)}), bf16[16,2,16,128]{3,2,1,0:T(8,128)(2,1)S(1)}, u32[]{:S(2)}, u32[]{:S(2)}) async-start(bf16[16,2,16,128]{3,2,1,0:T(8,128)(2,1)} %get-tuple-element.38), calls=%async_computation | async-start | bytes 262144 | tf_op jit(solution)/shard_map/all_to_all | solution.py:488
  92.0 8.0 %all-to-all-done.agg = bf16[16,2,16,128]{3,2,1,0:T(8,128)(2,1)S(1)} async-done(((bf16[16,2,16,128]{3,2,1,0:T(8,128)(2,1)}), bf16[16,2,16,128]{3,2,1,0:T(8,128)(2,1)S(1)}, u32[]{:S(2)}, u32[]{:S(2)}) %all-to-all-start) | async-done | bytes 131104 | tf_op jit(solution)/shard_map/all_to_all | solution.py:488
  102.1 11.1 %all_to_all.10.ragg = bf16[16,2,16,128]{3,2,1,0:T(8,128)(2,1)S(1)} all-to-all(bf16[16,2,16,128]{3,2,1,0:T(8,128)(2,1)S(1)} %get-tuple-element.48), channel_id=1, replica_groups={{0,16,32,48,64,80,96,112,128,144,160,176,192,208,224,240},{8,24,40,56,7..., dimensions={0} | all-to-all | bytes 262144 | tf_op jit(solution)/shard_map/all_to_all | solution.py:496
  113.2 4.8 %shard_map.84 = (bf16[128,1024]{1,0:T(8,128)(2,1)S(1)}, bf16[128,1024]{1,0:T(8,128)(2,1)S(1)}, bf16[256,768]{1,0:T(8,128)(2,1)S(1)}, f32[128,128]{1,0:T(8,128)S(1)}, f32[128,128]{1,0:T(8,128)S(1)}) custom-call(bf16[256,768]{1,0:T(8,128)(2,1)S(1)} %get-tuple-element.37.proj, f32[256,512]{1,0:T(8,128)S(1)} %get-tuple-element.47.gg, ...), custom_call_target="tpu_custom_call" | custom-call | tf_op jit(solution)/shard_map/pallas_call | solution.py:360
  117.9 5.1 %shard_map.85 = (bf16[3,128,1024]{2,1,0:T(8,128)(2,1)S(1)}, bf16[3,128,1024]{2,1,0:T(8,128)(2,1)S(1)}) custom-call(bf16[256,768]{1,0:T(8,128)(2,1)S(1)} %get-tuple-element.50.stk, bf16[16,2,3,128,256]{4,3,2,1,0:T(8,128)(2,1)} %get-tuple-element.49.wall), custom_call_target="tpu_custom_call" | custom-call | tf_op jit(solution)/shard_map/pallas_call | solution.py:360
  126.1 6.0 %collective-permute-start.28 = (bf16[128,1024]{1,0:T(8,128)(2,1)S(1)}, bf16[128,1024]{1,0:T(8,128)(2,1)S(1)}, u32[]{:S(2)}, u32[]{:S(2)}) collective-permute-start(bf16[128,1024]{1,0:T(8,128)(2,1)S(1)} %get-tuple-element.46), channel_id=1, source_target_pairs={{0,6},{2,0},{4,2},{6,4},{1,7},{3,1},{5,3},{7,5},{8,14},{10,8},{12,... | collective-permute-start | bytes 786440 | tf_op jit(solution)/shard_map/ppermute | solution.py:42
  132.5 4.4 %collective-permute-start.27 = (bf16[128,1024]{1,0:T(8,128)(2,1)S(1)}, bf16[128,1024]{1,0:T(8,128)(2,1)S(1)}, u32[]{:S(2)}, u32[]{:S(2)}) collective-permute-start(bf16[128,1024]{1,0:T(8,128)(2,1)S(1)} %shard_map.83), channel_id=1, source_target_pairs={{0,4},{2,6},{4,0},{6,2},{1,5},{3,7},{5,1},{7,3},{8,12},{10,14},{12... | collective-permute-start | bytes 786440 | tf_op jit(solution)/shard_map/ppermute | solution.py:42
  138.1 3.0 %collective-permute-start.31 = (bf16[128,1024]{1,0:T(8,128)(2,1)S(1)}, bf16[128,1024]{1,0:T(8,128)(2,1)S(1)}, u32[]{:S(2)}, u32[]{:S(2)}) collective-permute-start(bf16[128,1024]{1,0:T(8,128)(2,1)S(1)} %get-tuple-element.56), channel_id=1, source_target_pairs={{0,2},{2,4},{4,6},{6,0},{1,3},{3,5},{5,7},{7,1},{8,10},{10,12},{12... | collective-permute-start | bytes 786440 | tf_op jit(solution)/shard_map/ppermute | solution.py:42
  141.3 25.7 %collective-permute-done.27 = bf16[128,1024]{1,0:T(8,128)(2,1)S(1)} collective-permute-done((bf16[128,1024]{1,0:T(8,128)(2,1)S(1)}, bf16[128,1024]{1,0:T(8,128)(2,1)S(1)}, u32[]{:S(2)}, u32[]{:S(2)}) %collective-permute-start.27) | collective-permute-done | bytes 262176 | tf_op jit(solution)/shard_map/ppermute | solution.py:42
  167.9 4.7 %collective-permute-done.33.r2 = bf16[128,1024]{1,0:T(8,128)(2,1)S(1)} collective-permute-done((bf16[128,1024]{1,0:T(8,128)(2,1)S(1)}, bf16[128,1024]{1,0:T(8,128)(2,1)S(1)}, u32[]{:S(2)}, u32[]{:S(2)}) %collective-permute-start.33) | collective-permute-done | bytes 262176 | tf_op jit(solution)/shard_map/ppermute | solution.py:42
  172.6 9.1 %collective-permute-done.31.r1 = bf16[128,1024]{1,0:T(8,128)(2,1)S(1)} collective-permute-done((bf16[128,1024]{1,0:T(8,128)(2,1)S(1)}, bf16[128,1024]{1,0:T(8,128)(2,1)S(1)}, u32[]{:S(2)}, u32[]{:S(2)}) %collective-permute-start.31) | collective-permute-done | bytes 262176 | tf_op jit(solution)/shard_map/ppermute | solution.py:42
  (88 shorter events, 36.9 us)
Async XLA Ops:
  4.2 11.1 %collective-permute-start.4 = (bf16[2,3,128,256]{3,2,1,0:T(8,128)(2,1)S(1)}, bf16[2,3,128,256]{3,2,1,0:T(8,128)(2,1)S(1)}, u32[]{:S(2)}, u32[]{:S(2)}) collective-permute-start(bf16[2,3,128,256]{3,2,1,0:T(8,128)(2,1)S(1)} %get-tuple-element.63), channel_id=1, source_target_pairs={{0,16},{8,72},{16,32},{24,88},{32,48},{40,104},{48,0},{56,120},{64... | collective-permute-start | bytes 1179656 | tf_op jit(solution)/shard_map/ppermute | solution.py:438
  7.5 25.6 %collective-permute-start.9 = (bf16[2,3,128,256]{3,2,1,0:T(8,128)(2,1)S(1)}, bf16[2,3,128,256]{3,2,1,0:T(8,128)(2,1)S(1)}, u32[]{:S(2)}, u32[]{:S(2)}) collective-permute-start(bf16[2,3,128,256]{3,2,1,0:T(8,128)(2,1)S(1)} %get-tuple-element.63), channel_id=1, source_target_pairs={{0,64},{8,24},{16,80},{24,40},{32,96},{40,56},{48,112},{56,8},{64,... | collective-permute-start | bytes 1179656 | tf_op jit(solution)/shard_map/ppermute | solution.py:441
  11.6 15.6 %collective-permute-start = (bf16[136,1024]{1,0:T(8,128)(2,1)S(1)}, bf16[136,1024]{1,0:T(8,128)(2,1)S(1)}, u32[]{:S(2)}, u32[]{:S(2)}) collective-permute-start(bf16[136,1024]{1,0:T(8,128)(2,1)S(1)} %shard_map.77.p0.part), channel_id=1, source_target_pairs={{0,2},{2,4},{4,6},{6,0},{1,3},{3,5},{5,7},{7,1},{8,10},{10,12},{12... | collective-permute-start | bytes 835592 | tf_op jit(solution)/shard_map/ppermute | solution.py:42
  12.7 18.7 %collective-permute-start.1 = (bf16[136,1024]{1,0:T(8,128)(2,1)S(1)}, bf16[136,1024]{1,0:T(8,128)(2,1)S(1)}, u32[]{:S(2)}, u32[]{:S(2)}) collective-permute-start(bf16[136,1024]{1,0:T(8,128)(2,1)S(1)} %shard_map.77.p0.part), channel_id=1, source_target_pairs={{0,4},{2,6},{4,0},{6,2},{1,5},{3,7},{5,1},{7,3},{8,12},{10,14},{12... | collective-permute-start | bytes 835592 | tf_op jit(solution)/shard_map/ppermute | solution.py:42
  15.4 40.0 %collective-permute-start.11 = (bf16[2,2,3,128,256]{4,3,2,1,0:T(8,128)(2,1)S(1)}, bf16[2,2,3,128,256]{4,3,2,1,0:T(8,128)(2,1)S(1)}, u32[]{:S(2)}, u32[]{:S(2)}) collective-permute-start(bf16[2,2,3,128,256]{4,3,2,1,0:T(8,128)(2,1)S(1)} %pad_maximum_fusion.refs_1_), channel_id=1, source_target_pairs={{0,64},{8,24},{16,80},{24,40},{32,96},{40,56},{48,112},{56,8},{64,... | collective-permute-start | bytes 2359304 | tf_op jit(solution)/shard_map/ppermute | solution.py:441
  18.4 16.4 %collective-permute-start.5 = (bf16[1,3,128,256]{3,2,1,0:T(8,128)(2,1)S(1)}, bf16[1,3,128,256]{3,2,1,0:T(8,128)(2,1)S(1)}, u32[]{:S(2)}, u32[]{:S(2)}) collective-permute-start(bf16[1,3,128,256]{3,2,1,0:T(8,128)(2,1)S(1)} %slice.36), channel_id=1, source_target_pairs={{0,16},{8,72},{16,32},{24,88},{32,48},{40,104},{48,0},{56,120},{64... | collective-permute-start | bytes 589832 | tf_op jit(solution)/shard_map/ppermute | solution.py:438
  27.2 19.2 %collective-permute-start.10 = (bf16[2,3,128,256]{3,2,1,0:T(8,128)(2,1)S(1)}, bf16[2,3,128,256]{3,2,1,0:T(8,128)(2,1)S(1)}, u32[]{:S(2)}, u32[]{:S(2)}) collective-permute-start(bf16[2,3,128,256]{3,2,1,0:T(8,128)(2,1)S(1)} %get-tuple-element.63), channel_id=1, source_target_pairs={{0,192},{8,56},{16,208},{24,8},{32,224},{40,24},{48,240},{56,40},{... | collective-permute-start | bytes 1179656 | tf_op jit(solution)/shard_map/ppermute | solution.py:441
  33.2 22.7 %collective-permute-start.12 = (bf16[2,2,3,128,256]{4,3,2,1,0:T(8,128)(2,1)S(1)}, bf16[2,2,3,128,256]{4,3,2,1,0:T(8,128)(2,1)S(1)}, u32[]{:S(2)}, u32[]{:S(2)}) collective-permute-start(bf16[2,2,3,128,256]{4,3,2,1,0:T(8,128)(2,1)S(1)} %pad_maximum_fusion.refs_1_), channel_id=1, source_target_pairs={{0,192},{8,56},{16,208},{24,8},{32,224},{40,24},{48,240},{56,40},{... | collective-permute-start | bytes 2359304 | tf_op jit(solution)/shard_map/ppermute | solution.py:441
  47.3 29.3 %collective-permute-start.8 = (bf16[16,128,256]{2,1,0:T(8,128)(2,1)S(1)}, bf16[16,128,256]{2,1,0:T(8,128)(2,1)S(1)}, u32[]{:S(2)}, u32[]{:S(2)}) collective-permute-start(bf16[16,128,256]{2,1,0:T(8,128)(2,1)S(1)} %get-tuple-element.36.own), channel_id=1, source_target_pairs={{0,8},{8,0},{16,24},{24,16},{32,40},{40,32},{48,56},{56,48},{64,72... | collective-permute-start | bytes 3145736 | tf_op jit(solution)/shard_map/ppermute | solution.py:38
  52.2 13.8 %collective-permute-start.13 = (bf16[2,3,128,256]{3,2,1,0:T(8,128)(2,1)S(1)}, bf16[2,3,128,256]{3,2,1,0:T(8,128)(2,1)S(1)}, u32[]{:S(2)}, u32[]{:S(2)}) collective-permute-start(bf16[2,3,128,256]{3,2,1,0:T(8,128)(2,1)S(1)} %constant_dynamic-update-slice_fusion), channel_id=1, source_target_pairs={{0,64},{8,24},{16,80},{24,40},{32,96},{40,56},{48,112},{56,8},{64,... | collective-permute-start | bytes 1179656 | tf_op jit(solution)/shard_map/ppermute | solution.py:441
  52.6 16.2 %collective-permute-start.14 = (bf16[2,3,128,256]{3,2,1,0:T(8,128)(2,1)S(1)}, bf16[2,3,128,256]{3,2,1,0:T(8,128)(2,1)S(1)}, u32[]{:S(2)}, u32[]{:S(2)}) collective-permute-start(bf16[2,3,128,256]{3,2,1,0:T(8,128)(2,1)S(1)} %constant_dynamic-update-slice_fusion), channel_id=1, source_target_pairs={{0,192},{8,56},{16,208},{24,8},{32,224},{40,24},{48,240},{56,40},{... | collective-permute-start | bytes 1179656 | tf_op jit(solution)/shard_map/ppermute | solution.py:441
  55.9 14.8 %collective-permute-start.23 = (bf16[128,1024]{1,0:T(8,128)(2,1)S(1)}, bf16[128,1024]{1,0:T(8,128)(2,1)S(1)}, u32[]{:S(2)}, u32[]{:S(2)}) collective-permute-start(bf16[128,1024]{1,0:T(8,128)(2,1)S(1)} %bitcast.25), channel_id=1, source_target_pairs={{0,6},{2,0},{4,2},{6,4},{1,7},{3,1},{5,3},{7,5},{8,14},{10,8},{12,... | collective-permute-start | bytes 786440 | tf_op jit(solution)/shard_map/ppermute | solution.py:42
  65.5 11.1 %collective-permute-start.17 = (bf16[2,3,128,256]{3,2,1,0:T(8,128)(2,1)S(1)}, bf16[2,3,128,256]{3,2,1,0:T(8,128)(2,1)S(1)}, u32[]{:S(2)}, u32[]{:S(2)}) collective-permute-start(bf16[2,3,128,256]{3,2,1,0:T(8,128)(2,1)S(1)} %slice_bitcast_fusion.1), channel_id=1, source_target_pairs={{0,64},{8,24},{16,80},{24,40},{32,96},{40,56},{48,112},{56,8},{64,... | collective-permute-start | bytes 1179656 | tf_op jit(solution)/shard_map/ppermute | solution.py:441
  76.6 15.4 %collective-permute-start.24 = (f32[128,256]{1,0:T(8,128)S(1)}, f32[128,256]{1,0:T(8,128)S(1)}, u32[]{:S(2)}, u32[]{:S(2)}) collective-permute-start(f32[128,256]{1,0:T(8,128)S(1)} %get-tuple-element.41), channel_id=1, source_target_pairs={{0,8},{8,0},{16,24},{24,16},{32,40},{40,32},{48,56},{56,48},{64,72... | collective-permute-start | bytes 393224 | tf_op jit(solution)/shard_map/ppermute | solution.py:38
  86.1 13.9 %all-to-all-start = ((bf16[16,2,16,128]{3,2,1,0:T(8,128)(2,1)}), bf16[16,2,16,128]{3,2,1,0:T(8,128)(2,1)S(1)}, u32[]{:S(2)}, u32[]{:S(2)}) async-start(bf16[16,2,16,128]{3,2,1,0:T(8,128)(2,1)} %get-tuple-element.38), calls=%async_computation | async-start | bytes 262144 | tf_op jit(solution)/shard_map/all_to_all | solution.py:488
  123.1 14.6 %collective-permute-start.29 = (bf16[3,128,1024]{2,1,0:T(8,128)(2,1)S(1)}, bf16[3,128,1024]{2,1,0:T(8,128)(2,1)S(1)}, u32[]{:S(2)}, u32[]{:S(2)}) collective-permute-start(bf16[3,128,1024]{2,1,0:T(8,128)(2,1)S(1)} %get-tuple-element.52), channel_id=1, source_target_pairs={{0,8},{8,0},{16,24},{24,16},{32,40},{40,32},{48,56},{56,48},{64,72... | collective-permute-start | bytes 2359304 | tf_op jit(solution)/shard_map/ppermute | solution.py:38
  123.7 13.2 %collective-permute-start.30 = (f32[128,128]{1,0:T(8,128)S(1)}, f32[128,128]{1,0:T(8,128)S(1)}, u32[]{:S(2)}, u32[]{:S(2)}) collective-permute-start(f32[128,128]{1,0:T(8,128)S(1)} %get-tuple-element.55), channel_id=1, source_target_pairs={{0,8},{8,0},{16,24},{24,16},{32,40},{40,32},{48,56},{56,48},{64,72... | collective-permute-start | bytes 196616 | tf_op jit(solution)/shard_map/ppermute | solution.py:38
  123.8 13.1 %collective-permute-start.32 = (bf16[128,1024]{1,0:T(8,128)(2,1)S(1)}, bf16[128,1024]{1,0:T(8,128)(2,1)S(1)}, u32[]{:S(2)}, u32[]{:S(2)}) collective-permute-start(bf16[128,1024]{1,0:T(8,128)(2,1)S(1)} %get-tuple-element.58), channel_id=1, source_target_pairs={{0,8},{8,0},{16,24},{24,16},{32,40},{40,32},{48,56},{56,48},{64,72... | collective-permute-start | bytes 786440 | tf_op jit(solution)/shard_map/ppermute | solution.py:38
  126.1 15.1 %collective-permute-start.28 = (bf16[128,1024]{1,0:T(8,128)(2,1)S(1)}, bf16[128,1024]{1,0:T(8,128)(2,1)S(1)}, u32[]{:S(2)}, u32[]{:S(2)}) collective-permute-start(bf16[128,1024]{1,0:T(8,128)(2,1)S(1)} %get-tuple-element.46), channel_id=1, source_target_pairs={{0,6},{2,0},{4,2},{6,4},{1,7},{3,1},{5,3},{7,5},{8,14},{10,8},{12,... | collective-permute-start | bytes 786440 | tf_op jit(solution)/shard_map/ppermute | solution.py:42
  132.5 34.5 %collective-permute-start.27 = (bf16[128,1024]{1,0:T(8,128)(2,1)S(1)}, bf16[128,1024]{1,0:T(8,128)(2,1)S(1)}, u32[]{:S(2)}, u32[]{:S(2)}) collective-permute-start(bf16[128,1024]{1,0:T(8,128)(2,1)S(1)} %shard_map.83), channel_id=1, source_target_pairs={{0,4},{2,6},{4,0},{6,2},{1,5},{3,7},{5,1},{7,3},{8,12},{10,14},{12... | collective-permute-start | bytes 786440 | tf_op jit(solution)/shard_map/ppermute | solution.py:42
  136.9 30.1 %collective-permute-start.26 = (bf16[128,1024]{1,0:T(8,128)(2,1)S(1)}, bf16[128,1024]{1,0:T(8,128)(2,1)S(1)}, u32[]{:S(2)}, u32[]{:S(2)}) collective-permute-start(bf16[128,1024]{1,0:T(8,128)(2,1)S(1)} %get-tuple-element.45), channel_id=1, source_target_pairs={{0,2},{2,4},{4,6},{6,0},{1,3},{3,5},{5,7},{7,1},{8,10},{10,12},{12... | collective-permute-start | bytes 786440 | tf_op jit(solution)/shard_map/ppermute | solution.py:42
  137.1 35.6 %collective-permute-start.33 = (bf16[128,1024]{1,0:T(8,128)(2,1)S(1)}, bf16[128,1024]{1,0:T(8,128)(2,1)S(1)}, u32[]{:S(2)}, u32[]{:S(2)}) collective-permute-start(bf16[128,1024]{1,0:T(8,128)(2,1)S(1)} %shard_map.87), channel_id=1, source_target_pairs={{0,4},{2,6},{4,0},{6,2},{1,5},{3,7},{5,1},{7,3},{8,12},{10,14},{12... | collective-permute-start | bytes 786440 | tf_op jit(solution)/shard_map/ppermute | solution.py:42
  138.1 43.7 %collective-permute-start.31 = (bf16[128,1024]{1,0:T(8,128)(2,1)S(1)}, bf16[128,1024]{1,0:T(8,128)(2,1)S(1)}, u32[]{:S(2)}, u32[]{:S(2)}) collective-permute-start(bf16[128,1024]{1,0:T(8,128)(2,1)S(1)} %get-tuple-element.56), channel_id=1, source_target_pairs={{0,2},{2,4},{4,6},{6,0},{1,3},{3,5},{5,7},{7,1},{8,10},{10,12},{12... | collective-permute-start | bytes 786440 | tf_op jit(solution)/shard_map/ppermute | solution.py:42
  141.2 40.5 %collective-permute-start.34 = (bf16[128,1024]{1,0:T(8,128)(2,1)S(1)}, bf16[128,1024]{1,0:T(8,128)(2,1)S(1)}, u32[]{:S(2)}, u32[]{:S(2)}) collective-permute-start(bf16[128,1024]{1,0:T(8,128)(2,1)S(1)} %get-tuple-element.59), channel_id=1, source_target_pairs={{0,6},{2,0},{4,2},{6,4},{1,7},{3,1},{5,3},{7,5},{8,14},{10,8},{12,... | collective-permute-start | bytes 786440 | tf_op jit(solution)/shard_map/ppermute | solution.py:42
  (17 other events, 213.6 us)

commit v2 on v1

--- a/solution.py
+++ b/solution.py
@@ -80,10 +80,6 @@
 
 def slot_of(off):
     return jnp.where(off == 3, 1, jnp.where(off == 1, 2, jnp.where(off == 2, 3, 0)))
-
-
-def off_of(slot):
-    return jnp.where(slot == 1, 3, jnp.where(slot == 2, 1, jnp.where(slot == 3, 2, 0)))
 
 
 def within(proj, rows, h, mask):
@@ -99,10 +95,19 @@
     return qf, kf, v, rq, rk, kn, w
 
 
-def prepare_kernel(tokens, position, gain, message):
-    hidden = tokens[...].astype(F32) + position[...].astype(F32)[:, None, :]
+def prepare_kernel(tokens, position, gain, message, tok, pos, gn, sems):
+    copies = [
+        pltpu.make_async_copy(tokens, tok, sems.at[0]),
+        pltpu.make_async_copy(position, pos, sems.at[1]),
+        pltpu.make_async_copy(gain, gn, sems.at[2]),
+    ]
+    for copy in copies:
+        copy.start()
+    for copy in copies:
+        copy.wait()
+    hidden = tok[...].astype(F32) + pos[...].astype(F32)[:, None, :]
     message[0:128, :] = hidden.reshape(128, 1024).astype(BF)
-    message[128:136, :] = jnp.broadcast_to(gain[...], (8, 1024))
+    message[128:136, :] = jnp.broadcast_to(gn[...][None], (8, 1024))
 
 
 def norm_kernel(p0, p1, p2, p3, normed, inv):
@@ -121,17 +126,13 @@
             normed[n * 4 + b] = (h * r * g).astype(BF)
 
 
-PIECES = (
-    (0, 1), (1, 2), (3, 1), (4, 1), (8, 1), (5, 2), (9, 2), (7, 1), (11, 1),
-    (12, "a"), (12, "b"), (13, 1), (14, 1), (15, "a"), (15, "b"),
-)
-
-
-def project_kernel(own, oth, *refs):
-    pieces = refs[:15]
-    proj, agg, wall, wv, acc, sems, out_sems = refs[15:]
+EARLY = ((0, 1), (1, 2), (3, 1), (4, 1), (8, 1), (5, 2), (9, 2), (7, 1), (11, 1))
+LATE = ((0, "a"), (0, "b"), (1, 1), (2, 1), (3, "a"), (3, "b"))
+
+
+def load_pieces(pieces, places, wv, sems):
     copies = []
-    for n, (ref, (slot, size)) in enumerate(zip(pieces, PIECES)):
+    for n, (ref, (slot, size)) in enumerate(zip(pieces, places)):
         if size == "a":
             dst = wv.at[slot, 0:1]
         elif size == "b":
@@ -141,31 +142,54 @@
         copy = pltpu.make_async_copy(ref, dst, sems.at[n])
         copy.start()
         copies.append(copy)
+    return copies
+
+
+def group_lhs(own, oth, s3):
     y, x, core, z = place()
     lead = core == 0
-    acc[...] = jnp.zeros_like(acc)
-
-    def step(i, carry):
-        s3 = off_of(i // 4)
-        s1 = off_of(i % 4)
+    parts = []
+    for s1 in (0, 3, 1, 2):
         by = (y + jnp.where(lead, s3, s1)) % 4
         bx = (x + jnp.where(lead, s1, s3)) % 4
         blk = ((z + 4 - by) % 4) * 4 + bx
-        lhs = jnp.concatenate([own[blk], oth[blk]], 0)
+        parts.append(jnp.concatenate([own[blk], oth[blk]], 0))
+    return jnp.concatenate(parts, 1)
+
+
+def project_early_kernel(own, oth, *refs):
+    pieces = refs[:9]
+    acc, wall, wv, sems, out_sem = refs[9:]
+    copies = load_pieces(pieces, EARLY, wv, sems)
+    for n, group in enumerate(((0, 1, 2), (3, 5, 7), (4, 6, 8))):
+        for at in group:
+            copies[at].wait()
+        lhs = group_lhs(own, oth, (0, 3, 1)[n])
         for j in range(3):
-            w = wv[i, :, j].reshape(256, 256)
-            acc[:, j * 256:(j + 1) * 256] += dot_nn(lhs, w)
-        return carry
-
-    for copy in copies[:9]:
+            cols = slice(j * 256, (j + 1) * 256)
+            r = dot_nn(lhs, wv[n * 4:n * 4 + 4, :, j].reshape(1024, 256))
+            if n == 0:
+                acc[:, cols] = r
+            else:
+                acc[:, cols] += r
+    back = pltpu.make_async_copy(wv, wall.at[0:12], out_sem.at[0])
+    back.start()
+    back.wait()
+
+
+def project_late_kernel(own, oth, acc, wall_in, *refs):
+    pieces = refs[:6]
+    proj, agg, wall, wv, sems, out_sem = refs[6:]
+    copies = load_pieces(pieces, LATE, wv, sems)
+    lhs = group_lhs(own, oth, 2)
+    for copy in copies:
         copy.wait()
-    lax.fori_loop(0, 12, step, 0)
-    for copy in copies[9:]:
-        copy.wait()
-    back = pltpu.make_async_copy(wv, wall, out_sems.at[0])
+    back = pltpu.make_async_copy(wv, wall.at[12:16], out_sem.at[0])
     back.start()
-    lax.fori_loop(12, 16, step, 0)
-    proj[...] = acc[...].astype(BF)
+    for j in range(3):
+        cols = slice(j * 256, (j + 1) * 256)
+        r = dot_nn(lhs, wv[:, :, j].reshape(1024, 256))
+        proj[:, cols] = (acc[:, cols] + r).astype(BF)
     mask = same_patch(128, 128)
     for g in range(2):
         for h in range(2):
@@ -176,27 +200,39 @@
     back.wait()
 
 
-def across_kernel(proj, agg, gm, mix_own, mix_oth, gg, gagg):
+def across_kernel(proj, agg, mix_own, mix_oth, soft):
     mask = same_patch(256, 256)
     small = same_patch(128, 128)
     for h in range(2):
         cols = pl.ds(h * 128, 128)
         q = proj[:, cols]
-        qf = q.astype(F32)
+        rq = inv_norm(q.astype(F32))
+        a = agg[:, h].reshape(256, HD)
+        af = a.astype(F32)
+        an = (af * inv_norm(af)).astype(BF)
+        w = softmax_rows(dot_nt(q, an) * (rq * FAC), mask)
+        soft[h] = w
+        second = dot_nn(w.astype(BF), a)
+        for g, ref in enumerate((mix_own, mix_oth)):
+            fine = within(proj, pl.ds(g * 128, 128), h, small)
+            first = dot_nn(fine[6].astype(BF), fine[2])
+            ref[:, cols] = (first + second[g * 128:(g + 1) * 128]).astype(BF)
+
+
+def across_back_kernel(proj, agg, gm_mine, gm_got, soft, ow, gg, gagg, ow_near, sem):
+    copy = pltpu.make_async_copy(ow, ow_near, sem.at[0])
+    copy.start()
+    for h in range(2):
+        cols = pl.ds(h * 128, 128)
+        qf = proj[:, cols].astype(F32)
         rq = inv_norm(qf)
         a = agg[:, h].reshape(256, HD)
         af = a.astype(F32)
         ra = inv_norm(af)
         an = (af * ra).astype(BF)
-        s = dot_nt(q, an) * (rq * FAC)
-        w = softmax_rows(s, mask)
+        w = soft[h]
         wb = w.astype(BF)
-        second = dot_nn(wb, a)
-        for g, ref in enumerate((mix_own, mix_oth)):
-            fine = within(proj, pl.ds(g * 128, 128), h, small)
-            first = dot_nn(fine[6].astype(BF), fine[2])
-            ref[:, cols] = (first + second[g * 128:(g + 1) * 128]).astype(BF)
-        gf = gm[:, cols]
+        gf = jnp.concatenate([gm_mine[:, cols], gm_got[:, cols]], 0)
         g = gf.astype(BF)
         dw = dot_nt(g, a)
         ds = w * (dw - jnp.sum(w * dw, axis=-1, keepdims=True)) * FAC
@@ -206,6 +242,7 @@
         dan = dot_tn(dsb, (qf * rq).astype(BF))
         da = dot_tn(wb, g) + norm_back(af, ra, dan)
         gagg[:, h] = da.astype(BF).reshape(16, 16, HD)
+    copy.wait()
 
 
 def quarter_slots(d):
@@ -229,10 +266,8 @@
 
 
 def block_product(stk, wv, n):
-    r = jnp.zeros((256, 256), F32)
-    for j in range(3):
-        r = r + dot_nt(stk[:, j * 256:(j + 1) * 256], wv[n, :, j].reshape(256, 256))
-    return r
+    w = jnp.concatenate([wv[n, :, j].reshape(256, 256) for j in range(3)], 1)
+    return dot_nt(stk[...], w)
 
 
 def back_kernel(proj, gg, ragg, wall, own, oth, stk, corr_own, corr_oth, wv, sems):
@@ -370,8 +405,19 @@
 BLOCK = (2, 3, 128, 256)
 
 
+def in_hbm(value):
+    return pltpu.with_memory_space_constraint(value, pltpu.HBM)
+
+
 def prepare(tokens, position, gain):
-    return call(prepare_kernel, [VM] * 3, [(VM, shape((136, 1024), BF))], (tokens, position, gain))[0]
+    return call(
+        prepare_kernel, [HB] * 3, [(VM, shape((136, 1024), BF))],
+        (in_hbm(tokens), in_hbm(position), in_hbm(gain)),
+        (
+            pltpu.VMEM((16, 8, 1024), BF), pltpu.VMEM((16, 1024), BF), pltpu.VMEM((1024,), BF),
+            pltpu.SemaphoreType.DMA((3,)),
+        ),
+    )[0]
 
 
 def normalise(parts):
@@ -381,26 +427,45 @@
     )
 
 
-def project(own, oth, weights):
+WALL = pltpu.HBM((16,) + BLOCK, BF)
+
+
+def project_early(own, oth, weights):
     return call(
-        project_kernel, [VM, VM] + [AN] * 15,
-        [(VM, shape((256, 768), BF)), (VM, shape((16, 2, 16, HD), BF)), (HB, pltpu.HBM((16,) + BLOCK, BF))],
+        project_early_kernel, [VM, VM] + [AN] * 9,
+        [(VM, shape((256, 768), F32)), (HB, WALL)],
         (own, oth) + weights,
-        (
-            pltpu.VMEM((16,) + BLOCK, BF), pltpu.VMEM((256, 768), F32),
-            pltpu.SemaphoreType.DMA((15,)), pltpu.SemaphoreType.DMA((1,)),
-        ),
-    )
-
-
-def across(proj, agg, gm):
+        (pltpu.VMEM((12,) + BLOCK, BF), pltpu.SemaphoreType.DMA((9,)), pltpu.SemaphoreType.DMA((1,))),
+    )
+
+
+def project_late(own, oth, acc, wall, weights):
+    return pl.pallas_call(
+        project_late_kernel,
+        in_specs=[VM, VM, VM, HB] + [AN] * 6,
+        out_specs=[VM, VM, HB],
+        out_shape=[shape((256, 768), BF), shape((16, 2, 16, HD), BF), WALL],
+        scratch_shapes=[pltpu.VMEM((4,) + BLOCK, BF), pltpu.SemaphoreType.DMA((6,)), pltpu.SemaphoreType.DMA((1,))],
+        input_output_aliases={3: 2},
+        compiler_params=PARAMS,
+        name="late",
+    )(own, oth, acc, in_hbm(wall), *weights)
+
+
+def across(proj, agg):
     return call(
-        across_kernel, [VM] * 3,
-        [
-            (VM, shape((128, 256), BF)), (VM, shape((128, 256), BF)),
-            (VM, shape((256, 512), F32)), (VM, shape((16, 2, 16, HD), BF)),
-        ],
-        (proj, agg, gm),
+        across_kernel, [VM] * 2,
+        [(VM, shape((128, 256), BF)), (VM, shape((128, 256), BF)), (VM, shape((2, 256, 256), F32))],
+        (proj, agg),
+    )
+
+
+def across_back(proj, agg, gm_mine, gm_got, soft, out_weight):
+    return call(
+        across_back_kernel, [VM] * 5 + [HB],
+        [(VM, shape((256, 512), F32)), (VM, shape((16, 2, 16, HD), BF)), (VM, shape((512, 4096), BF))],
+        (proj, agg, gm_mine, gm_got, soft, in_hbm(out_weight)),
+        (pltpu.SemaphoreType.DMA((1,)),),
     )
 
 
@@ -411,7 +476,7 @@
             (VM, shape((128, 1024), BF)), (VM, shape((128, 1024), BF)), (VM, shape((256, 768), BF)),
             (VM, shape((128, 128), F32)), (VM, shape((128, 128), F32)),
         ],
-        (proj, gg, ragg, pltpu.with_memory_space_constraint(wall, pltpu.HBM)),
+        (proj, gg, ragg, in_hbm(wall)),
         (pltpu.VMEM((4,) + BLOCK, BF), pltpu.SemaphoreType.DMA((4,))),
     )
 
@@ -420,7 +485,7 @@
     return call(
         rest_kernel, [VM, HB],
         [(VM, shape((3, 128, 1024), BF)), (VM, shape((3, 128, 1024), BF))],
-        (stk, pltpu.with_memory_space_constraint(wall, pltpu.HBM)),
+        (stk, in_hbm(wall)),
         (pltpu.VMEM((12,) + BLOCK, BF), pltpu.SemaphoreType.DMA((12,))),
     )
 
@@ -442,10 +507,10 @@
 
     r = near(own, 1)
     l = near(own, -1)
+
     up = cross(own, 1)
     down = cross(own, -1)
     pair = jnp.stack([r, l])
-
     far = jnp.concatenate([near(r[:1], 1), near(l[1:], -1)], 0)
     pair_up = cross(pair, 1)
     pair_down = cross(pair, -1)
@@ -463,18 +528,18 @@
 
     lead = tuple(whole(v) for v in (own, pair, far, up, down, pair_up, pair_down, far_up, far_down))
     tail = (over_a, over_b, whole(pair_a), whole(pair_b), far_a, far_b)
-    return lead + tail, far
+    return lead, tail, far
 
 
 def layer(tokens, position, gain, qkv_weight, out_weight, cotangent):
     _, _, core, _ = place()
 
     own_w = own_weights(qkv_weight, core)
-    message = prepare(tokens, position, gain.reshape(1, 1024))
+    message = prepare(tokens, position, gain)
     h_parts = [message]
     for d in (1, 2, 3):
         h_parts.append(zshift(message, d))
-    weights, far = gather_weights(own_w)
+    early, late, far = gather_weights(own_w)
 
     waited, _ = lax.optimization_barrier((h_parts, far))
     normed, inv_rms = normalise(waited)
@@ -484,26 +549,28 @@
     for d in (1, 2, 3):
         c_parts.append(zshift(cot_b, d))
     normed_other = swap(normed)
-    proj, agg, wall = project(normed, normed_other, weights)
+    acc, wall = project_early(normed, normed_other, early)
+    proj, agg, wall = project_late(normed, normed_other, acc, wall, late)
     agg_all = lax.all_to_all(agg, "chan", 0, 0, axis_index_groups=SAME_CORE, tiled=True)
 
     gm_mine, gm_other = call(
         gm_kernel, [VM] * 5, [(VM, shape((128, 256), F32))] * 2, c_parts + [out_weight],
     )
-    gm = jnp.concatenate([gm_mine, swap(gm_other)], 0)
-
-    mix_own, mix_oth, gg, gagg = across(proj, agg_all, gm)
+    gm_got = swap(gm_other)
+
+    mix_own, mix_oth, soft = across(proj, agg_all)
+    mix_got = swap(mix_oth)
+    gg, gagg, ow_near = across_back(proj, agg_all, gm_mine, gm_got, soft, out_weight)
     ragg = lax.all_to_all(gagg, "chan", 0, 0, axis_index_groups=SAME_CORE, tiled=True)
 
-    mix_got = swap(mix_oth)
     o2, = call(
-        out_first_kernel, [VM] * 3, [(VM, shape((128, 1024), BF))], (mix_own, mix_got, out_weight),
+        out_first_kernel, [VM] * 3, [(VM, shape((128, 1024), BF))], (mix_own, mix_got, ow_near),
     )
     s2 = zshift(o2, 2)
     o1, o3, o0 = call(
         out_rest_kernel, [VM] * 3,
         [(VM, shape((128, 1024), BF)), (VM, shape((128, 1024), BF)), (VM, shape((128, 1024), F32))],
-        (mix_own, mix_got, out_weight),
+        (mix_own, mix_got, ow_near),
     )
     s1 = zshift(o1, 1)
     s3 = zshift(o3, 3)

time: 183 us -> 171 us (0.934)
  the two profiles are of different devices: /device:TPU:192 before, /device:TPU:65 now
where the time goes in v2:
time: 171 us; the launch traced here: 170 us
  waiting for transfers between devices  69.8 us (41%)
  starting transfers between devices  49.1 us (29%)
  Pallas kernels  27.6 us (16%)
  blocking collectives  19.6 us (11%)
  other arithmetic  2.21 us (1%)
    ppermute x12, waiting for transfers between devices, zshift(): lax.ppermute(value, 'head', [(i, (i + step) % NZ) for i in range(NZ)])  65.8 us
    ppermute x12, starting transfers between devices, zshift(): lax.ppermute(value, 'head', [(i, (i + step) % NZ) for i in range(NZ)])  24.5 us
    pallas_call x13, Pallas kernels, call(): pl.pallas_call(kernel, in_specs=ins, out_specs=[spec for spec, _ in outs]...  24.4 us
    ppermute x12, starting transfers between devices, cross(): return lax.ppermute(value, 'chan', ring(False, step))  13.5 us
    all_to_all x1, blocking collectives, layer(): lax.all_to_all(agg, 'chan', 0, 0, axis_index_groups=SAME_CORE, tiled=True)  9.88 us
    all_to_all x1, blocking collectives, layer(): lax.all_to_all(gagg, 'chan', 0, 0, axis_index_groups=SAME_CORE, tiled=True)  9.67 us
    ppermute x7, starting transfers between devices, swap(): return lax.ppermute(value, 'chan', SWAP)  7.5 us
    ppermute x4, starting transfers between devices, near(): return lax.ppermute(value, 'chan', ring(True, step))  3.48 us
  transfers between devices with their start and end apart: 35, of which 15 were waited for; matrix products, arithmetic and copies ran while one was open for 1% of the time, Pallas kernels for 8%

profile of v2, /device:TPU:65, one launch (start us, length us, event | category | flops | bytes accessed | tf_op | source)
XLA Modules:
  0.0 170.3 jit_solution(11925924106905807735)
XLA Ops:
  13.5 2.5 %collective-permute-start.11 = (bf16[2,2,3,128,256]{4,3,2,1,0:T(8,128)(2,1)S(1)}, bf16[2,2,3,128,256]{4,3,2,1,0:T(8,128)(2,1)S(1)}, u32[]{:S(2)}, u32[]{:S(2)}) collective-permute-start(bf16[2,2,3,128,256]{4,3,2,1,0:T(8,128)(2,1)S(1)} %pad_maximum_fusion.refs_1_), channel_id=1, source_target_pairs={{0,64},{8,24},{16,80},{24,40},{32,96},{40,56},{48,112},{56,8},{64,... | collective-permute-start | bytes 2359304 | tf_op jit(solution)/shard_map/ppermute | solution.py:506
  17.2 2.5 %collective-permute-start.1 = (bf16[136,1024]{1,0:T(8,128)(2,1)S(1)}, bf16[136,1024]{1,0:T(8,128)(2,1)S(1)}, u32[]{:S(2)}, u32[]{:S(2)}) collective-permute-start(bf16[136,1024]{1,0:T(8,128)(2,1)S(1)} %shard_map.77.p0.part), channel_id=1, source_target_pairs={{0,4},{2,6},{4,0},{6,2},{1,5},{3,7},{5,1},{7,3},{8,12},{10,14},{12... | collective-permute-start | bytes 835592 | tf_op jit(solution)/shard_map/ppermute | solution.py:42
  19.8 2.6 %collective-permute-start.12 = (bf16[2,2,3,128,256]{4,3,2,1,0:T(8,128)(2,1)S(1)}, bf16[2,2,3,128,256]{4,3,2,1,0:T(8,128)(2,1)S(1)}, u32[]{:S(2)}, u32[]{:S(2)}) collective-permute-start(bf16[2,2,3,128,256]{4,3,2,1,0:T(8,128)(2,1)S(1)} %pad_maximum_fusion.refs_1_), channel_id=1, source_target_pairs={{0,192},{8,56},{16,208},{24,8},{32,224},{40,24},{48,240},{56,40},{... | collective-permute-start | bytes 2359304 | tf_op jit(solution)/shard_map/ppermute | solution.py:506
  23.3 7.7 %collective-permute-done.1.p2.part = bf16[136,1024]{1,0:T(8,128)(2,1)S(1)} collective-permute-done((bf16[136,1024]{1,0:T(8,128)(2,1)S(1)}, bf16[136,1024]{1,0:T(8,128)(2,1)S(1)}, u32[]{:S(2)}, u32[]{:S(2)}) %collective-permute-start.1) | collective-permute-done | bytes 278560 | tf_op jit(solution)/shard_map/ppermute | solution.py:42
  31.0 2.4 %collective-permute-start.15 = (bf16[1,3,128,256]{3,2,1,0:T(8,128)(2,1)S(1)}, bf16[1,3,128,256]{3,2,1,0:T(8,128)(2,1)S(1)}, u32[]{:S(2)}, u32[]{:S(2)}) collective-permute-start(bf16[1,3,128,256]{3,2,1,0:T(8,128)(2,1)S(1)} %slice.38), channel_id=1, source_target_pairs={{0,64},{8,24},{16,80},{24,40},{32,96},{40,56},{48,112},{56,8},{64,... | collective-permute-start | bytes 589832 | tf_op jit(solution)/shard_map/ppermute | solution.py:506
  33.7 3.3 %collective-permute-done.2.p3.part_a = bf16[136,1024]{1,0:T(8,128)(2,1)S(1)} collective-permute-done((bf16[136,1024]{1,0:T(8,128)(2,1)S(1)}, bf16[136,1024]{1,0:T(8,128)(2,1)S(1)}, u32[]{:S(2)}, u32[]{:S(2)}) %collective-permute-start.2) | collective-permute-done | bytes 278560 | tf_op jit(solution)/shard_map/ppermute | solution.py:42
  38.1 8.0 %collective-permute-start.22 = (bf16[128,1024]{1,0:T(8,128)(2,1)S(1)}, bf16[128,1024]{1,0:T(8,128)(2,1)S(1)}, u32[]{:S(2)}, u32[]{:S(2)}) collective-permute-start(bf16[128,1024]{1,0:T(8,128)(2,1)S(1)} %bitcast.23), channel_id=1, source_target_pairs={{0,2},{2,4},{4,6},{6,0},{1,3},{3,5},{5,7},{7,1},{8,10},{10,12},{12... | collective-permute-start | bytes 786440 | tf_op jit(solution)/shard_map/ppermute | solution.py:42
  47.5 2.8 %collective-permute-done.22.c1 = bf16[128,1024]{1,0:T(8,128)(2,1)S(1)} collective-permute-done((bf16[128,1024]{1,0:T(8,128)(2,1)S(1)}, bf16[128,1024]{1,0:T(8,128)(2,1)S(1)}, u32[]{:S(2)}, u32[]{:S(2)}) %collective-permute-start.22) | collective-permute-done | bytes 262176 | tf_op jit(solution)/shard_map/ppermute | solution.py:42
  50.4 3.1 %collective-permute-start.23 = (bf16[128,1024]{1,0:T(8,128)(2,1)S(1)}, bf16[128,1024]{1,0:T(8,128)(2,1)S(1)}, u32[]{:S(2)}, u32[]{:S(2)}) collective-permute-start(bf16[128,1024]{1,0:T(8,128)(2,1)S(1)} %bitcast.24), channel_id=1, source_target_pairs={{0,4},{2,6},{4,0},{6,2},{1,5},{3,7},{5,1},{7,3},{8,12},{10,14},{12... | collective-permute-start | bytes 786440 | tf_op jit(solution)/shard_map/ppermute | solution.py:42
  56.6 7.3 %collective-permute-done.23.c2 = bf16[128,1024]{1,0:T(8,128)(2,1)S(1)} collective-permute-done((bf16[128,1024]{1,0:T(8,128)(2,1)S(1)}, bf16[128,1024]{1,0:T(8,128)(2,1)S(1)}, u32[]{:S(2)}, u32[]{:S(2)}) %collective-permute-start.23) | collective-permute-done | bytes 262176 | tf_op jit(solution)/shard_map/ppermute | solution.py:42
  63.9 5.6 %collective-permute-done.24.c3 = bf16[128,1024]{1,0:T(8,128)(2,1)S(1)} collective-permute-done((bf16[128,1024]{1,0:T(8,128)(2,1)S(1)}, bf16[128,1024]{1,0:T(8,128)(2,1)S(1)}, u32[]{:S(2)}, u32[]{:S(2)}) %collective-permute-start.24) | collective-permute-done | bytes 262176 | tf_op jit(solution)/shard_map/ppermute | solution.py:42
  71.0 2.9 %collective-permute-start.25 = (f32[128,256]{1,0:T(8,128)S(1)}, f32[128,256]{1,0:T(8,128)S(1)}, u32[]{:S(2)}, u32[]{:S(2)}) collective-permute-start(f32[128,256]{1,0:T(8,128)S(1)} %get-tuple-element.49), channel_id=1, source_target_pairs={{0,8},{8,0},{16,24},{24,16},{32,40},{40,32},{48,56},{56,48},{64,72... | collective-permute-start | bytes 393224 | tf_op jit(solution)/shard_map/ppermute | solution.py:38
  73.9 5.4 %shard_map.79 = (f32[256,768]{1,0:T(8,128)S(1)}, bf16[16,2,3,128,256]{4,3,2,1,0:T(8,128)(2,1)}) custom-call(bf16[16,128,256]{2,1,0:T(8,128)(2,1)S(1)} %get-tuple-element.40.own, bf16[16,128,256]{2,1,0:T(8,128)(2,1)S(1)} %collective-permute-done.8.oth, bf16[1,2,3,128,256]{4,3,2,1,0:T(8,128)(2,1)S(1)} %get-tuple-element.70.refs_0_, ...), custom_call_target="tpu_custom_call" | custom-call | tf_op jit(solution)/shard_map/pallas_call | solution.py:395
  79.4 3.1 %late.1 = (bf16[256,768]{1,0:T(8,128)(2,1)S(1)}, bf16[16,2,16,128]{3,2,1,0:T(8,128)(2,1)S(1)}, bf16[16,2,3,128,256]{4,3,2,1,0:T(8,128)(2,1)}) custom-call(bf16[16,128,256]{2,1,0:T(8,128)(2,1)S(1)} %get-tuple-element.40.own, bf16[16,128,256]{2,1,0:T(8,128)(2,1)S(1)} %collective-permute-done.8.oth, ...), custom_call_target="tpu_custom_call", output_to_operand_aliasing={{2}: (3, {})} | custom-call | tf_op jit(solution)/shard_map/late/pallas_call | solution.py:443
  82.5 9.9 %all_to_all.10.agg = bf16[16,2,16,128]{3,2,1,0:T(8,128)(2,1)S(1)} all-to-all(bf16[16,2,16,128]{3,2,1,0:T(8,128)(2,1)S(1)} %get-tuple-element.44), channel_id=1, replica_groups={{0,16,32,48,64,80,96,112,128,144,160,176,192,208,224,240},{8,24,40,56,7..., dimensions={0} | all-to-all | bytes 262144 | tf_op jit(solution)/shard_map/all_to_all | solution.py:554
  96.0 9.7 %all_to_all.11.ragg = bf16[16,2,16,128]{3,2,1,0:T(8,128)(2,1)S(1)} all-to-all(bf16[16,2,16,128]{3,2,1,0:T(8,128)(2,1)S(1)} %get-tuple-element.56), channel_id=1, replica_groups={{0,16,32,48,64,80,96,112,128,144,160,176,192,208,224,240},{8,24,40,56,7..., dimensions={0} | all-to-all | bytes 262144 | tf_op jit(solution)/shard_map/all_to_all | solution.py:564
  105.7 4.8 %shard_map.85 = (bf16[128,1024]{1,0:T(8,128)(2,1)S(1)}, bf16[128,1024]{1,0:T(8,128)(2,1)S(1)}, bf16[256,768]{1,0:T(8,128)(2,1)S(1)}, f32[128,128]{1,0:T(8,128)S(1)}, f32[128,128]{1,0:T(8,128)S(1)}) custom-call(bf16[256,768]{1,0:T(8,128)(2,1)S(1)} %get-tuple-element.43.proj, f32[256,512]{1,0:T(8,128)S(1)} %get-tuple-element.55.gg, ...), custom_call_target="tpu_custom_call" | custom-call | tf_op jit(solution)/shard_map/pallas_call | solution.py:395
  110.5 5.1 %shard_map.86 = (bf16[3,128,1024]{2,1,0:T(8,128)(2,1)S(1)}, bf16[3,128,1024]{2,1,0:T(8,128)(2,1)S(1)}) custom-call(bf16[256,768]{1,0:T(8,128)(2,1)S(1)} %get-tuple-element.58.stk, bf16[16,2,3,128,256]{4,3,2,1,0:T(8,128)(2,1)} %get-tuple-element.57.wall), custom_call_target="tpu_custom_call" | custom-call | tf_op jit(solution)/shard_map/pallas_call | solution.py:395
  115.6 2.6 %collective-permute-start.29 = (bf16[3,128,1024]{2,1,0:T(8,128)(2,1)S(1)}, bf16[3,128,1024]{2,1,0:T(8,128)(2,1)S(1)}, u32[]{:S(2)}, u32[]{:S(2)}) collective-permute-start(bf16[3,128,1024]{2,1,0:T(8,128)(2,1)S(1)} %get-tuple-element.60), channel_id=1, source_target_pairs={{0,8},{8,0},{16,24},{24,16},{32,40},{40,32},{48,56},{56,48},{64,72... | collective-permute-start | bytes 2359304 | tf_op jit(solution)/shard_map/ppermute | solution.py:38
  121.3 4.6 %collective-permute-start.26 = (bf16[128,1024]{1,0:T(8,128)(2,1)S(1)}, bf16[128,1024]{1,0:T(8,128)(2,1)S(1)}, u32[]{:S(2)}, u32[]{:S(2)}) collective-permute-start(bf16[128,1024]{1,0:T(8,128)(2,1)S(1)} %get-tuple-element.53), channel_id=1, source_target_pairs={{0,2},{2,4},{4,6},{6,0},{1,3},{3,5},{5,7},{7,1},{8,10},{10,12},{12... | collective-permute-start | bytes 786440 | tf_op jit(solution)/shard_map/ppermute | solution.py:42
  130.4 6.9 %collective-permute-done.27 = bf16[128,1024]{1,0:T(8,128)(2,1)S(1)} collective-permute-done((bf16[128,1024]{1,0:T(8,128)(2,1)S(1)}, bf16[128,1024]{1,0:T(8,128)(2,1)S(1)}, u32[]{:S(2)}, u32[]{:S(2)}) %collective-permute-start.27) | collective-permute-done | bytes 262176 | tf_op jit(solution)/shard_map/ppermute | solution.py:42
  137.3 15.6 %collective-permute-done.26 = bf16[128,1024]{1,0:T(8,128)(2,1)S(1)} collective-permute-done((bf16[128,1024]{1,0:T(8,128)(2,1)S(1)}, bf16[128,1024]{1,0:T(8,128)(2,1)S(1)}, u32[]{:S(2)}, u32[]{:S(2)}) %collective-permute-start.26) | collective-permute-done | bytes 262176 | tf_op jit(solution)/shard_map/ppermute | solution.py:42
  155.0 5.0 %collective-permute-done.33.r2 = bf16[128,1024]{1,0:T(8,128)(2,1)S(1)} collective-permute-done((bf16[128,1024]{1,0:T(8,128)(2,1)S(1)}, bf16[128,1024]{1,0:T(8,128)(2,1)S(1)}, u32[]{:S(2)}, u32[]{:S(2)}) %collective-permute-start.33) | collective-permute-done | bytes 262176 | tf_op jit(solution)/shard_map/ppermute | solution.py:42
  160.0 9.2 %collective-permute-done.31.r1 = bf16[128,1024]{1,0:T(8,128)(2,1)S(1)} collective-permute-done((bf16[128,1024]{1,0:T(8,128)(2,1)S(1)}, bf16[128,1024]{1,0:T(8,128)(2,1)S(1)}, u32[]{:S(2)}, u32[]{:S(2)}) %collective-permute-start.31) | collective-permute-done | bytes 262176 | tf_op jit(solution)/shard_map/ppermute | solution.py:42
  (81 shorter events, 36.6 us)
Async XLA Ops:
  7.6 12.2 %collective-permute-start.9 = (bf16[2,3,128,256]{3,2,1,0:T(8,128)(2,1)S(1)}, bf16[2,3,128,256]{3,2,1,0:T(8,128)(2,1)S(1)}, u32[]{:S(2)}, u32[]{:S(2)}) collective-permute-start(bf16[2,3,128,256]{3,2,1,0:T(8,128)(2,1)S(1)} %get-tuple-element.71), channel_id=1, source_target_pairs={{0,64},{8,24},{16,80},{24,40},{32,96},{40,56},{48,112},{56,8},{64,... | collective-permute-start | bytes 1179656 | tf_op jit(solution)/shard_map/ppermute | solution.py:506
  11.6 10.8 %collective-permute-start.10 = (bf16[2,3,128,256]{3,2,1,0:T(8,128)(2,1)S(1)}, bf16[2,3,128,256]{3,2,1,0:T(8,128)(2,1)S(1)}, u32[]{:S(2)}, u32[]{:S(2)}) collective-permute-start(bf16[2,3,128,256]{3,2,1,0:T(8,128)(2,1)S(1)} %get-tuple-element.71), channel_id=1, source_target_pairs={{0,192},{8,56},{16,208},{24,8},{32,224},{40,24},{48,240},{56,40},{... | collective-permute-start | bytes 1179656 | tf_op jit(solution)/shard_map/ppermute | solution.py:506
  13.5 33.6 %collective-permute-start.11 = (bf16[2,2,3,128,256]{4,3,2,1,0:T(8,128)(2,1)S(1)}, bf16[2,2,3,128,256]{4,3,2,1,0:T(8,128)(2,1)S(1)}, u32[]{:S(2)}, u32[]{:S(2)}) collective-permute-start(bf16[2,2,3,128,256]{4,3,2,1,0:T(8,128)(2,1)S(1)} %pad_maximum_fusion.refs_1_), channel_id=1, source_target_pairs={{0,64},{8,24},{16,80},{24,40},{32,96},{40,56},{48,112},{56,8},{64,... | collective-permute-start | bytes 2359304 | tf_op jit(solution)/shard_map/ppermute | solution.py:506
  17.2 13.7 %collective-permute-start.1 = (bf16[136,1024]{1,0:T(8,128)(2,1)S(1)}, bf16[136,1024]{1,0:T(8,128)(2,1)S(1)}, u32[]{:S(2)}, u32[]{:S(2)}) collective-permute-start(bf16[136,1024]{1,0:T(8,128)(2,1)S(1)} %shard_map.77.p0.part), channel_id=1, source_target_pairs={{0,4},{2,6},{4,0},{6,2},{1,5},{3,7},{5,1},{7,3},{8,12},{10,14},{12... | collective-permute-start | bytes 835592 | tf_op jit(solution)/shard_map/ppermute | solution.py:42
  19.8 33.7 %collective-permute-start.12 = (bf16[2,2,3,128,256]{4,3,2,1,0:T(8,128)(2,1)S(1)}, bf16[2,2,3,128,256]{4,3,2,1,0:T(8,128)(2,1)S(1)}, u32[]{:S(2)}, u32[]{:S(2)}) collective-permute-start(bf16[2,2,3,128,256]{4,3,2,1,0:T(8,128)(2,1)S(1)} %pad_maximum_fusion.refs_1_), channel_id=1, source_target_pairs={{0,192},{8,56},{16,208},{24,8},{32,224},{40,24},{48,240},{56,40},{... | collective-permute-start | bytes 2359304 | tf_op jit(solution)/shard_map/ppermute | solution.py:506
  22.4 11.0 %collective-permute-start.7 = (bf16[1,3,128,256]{3,2,1,0:T(8,128)(2,1)S(1)}, bf16[1,3,128,256]{3,2,1,0:T(8,128)(2,1)S(1)}, u32[]{:S(2)}, u32[]{:S(2)}) collective-permute-start(bf16[1,3,128,256]{3,2,1,0:T(8,128)(2,1)S(1)} %slice.37), channel_id=1, source_target_pairs={{0,48},{8,200},{16,0},{24,216},{32,16},{40,232},{48,32},{56,248},{... | collective-permute-start | bytes 589832 | tf_op jit(solution)/shard_map/ppermute | solution.py:503
  22.9 14.0 %collective-permute-start.2 = (bf16[136,1024]{1,0:T(8,128)(2,1)S(1)}, bf16[136,1024]{1,0:T(8,128)(2,1)S(1)}, u32[]{:S(2)}, u32[]{:S(2)}) collective-permute-start(bf16[136,1024]{1,0:T(8,128)(2,1)S(1)} %shard_map.77.p0.part), channel_id=1, source_target_pairs={{0,6},{2,0},{4,2},{6,4},{1,7},{3,1},{5,3},{7,5},{8,14},{10,8},{12,... | collective-permute-start | bytes 835592 | tf_op jit(solution)/shard_map/ppermute | solution.py:42
  33.4 12.6 %collective-permute-start.16 = (bf16[1,3,128,256]{3,2,1,0:T(8,128)(2,1)S(1)}, bf16[1,3,128,256]{3,2,1,0:T(8,128)(2,1)S(1)}, u32[]{:S(2)}, u32[]{:S(2)}) collective-permute-start(bf16[1,3,128,256]{3,2,1,0:T(8,128)(2,1)S(1)} %slice.39), channel_id=1, source_target_pairs={{0,192},{8,56},{16,208},{24,8},{32,224},{40,24},{48,240},{56,40},{... | collective-permute-start | bytes 589832 | tf_op jit(solution)/shard_map/ppermute | solution.py:506
  37.5 33.6 %collective-permute-start.8 = (bf16[16,128,256]{2,1,0:T(8,128)(2,1)S(1)}, bf16[16,128,256]{2,1,0:T(8,128)(2,1)S(1)}, u32[]{:S(2)}, u32[]{:S(2)}) collective-permute-start(bf16[16,128,256]{2,1,0:T(8,128)(2,1)S(1)} %get-tuple-element.40.own), channel_id=1, source_target_pairs={{0,8},{8,0},{16,24},{24,16},{32,40},{40,32},{48,56},{56,48},{64,72... | collective-permute-start | bytes 3145736 | tf_op jit(solution)/shard_map/ppermute | solution.py:38
  38.1 12.3 %collective-permute-start.22 = (bf16[128,1024]{1,0:T(8,128)(2,1)S(1)}, bf16[128,1024]{1,0:T(8,128)(2,1)S(1)}, u32[]{:S(2)}, u32[]{:S(2)}) collective-permute-start(bf16[128,1024]{1,0:T(8,128)(2,1)S(1)} %bitcast.23), channel_id=1, source_target_pairs={{0,2},{2,4},{4,6},{6,0},{1,3},{3,5},{5,7},{7,1},{8,10},{10,12},{12... | collective-permute-start | bytes 786440 | tf_op jit(solution)/shard_map/ppermute | solution.py:42
  50.4 13.5 %collective-permute-start.23 = (bf16[128,1024]{1,0:T(8,128)(2,1)S(1)}, bf16[128,1024]{1,0:T(8,128)(2,1)S(1)}, u32[]{:S(2)}, u32[]{:S(2)}) collective-permute-start(bf16[128,1024]{1,0:T(8,128)(2,1)S(1)} %bitcast.24), channel_id=1, source_target_pairs={{0,4},{2,6},{4,0},{6,2},{1,5},{3,7},{5,1},{7,3},{8,12},{10,14},{12... | collective-permute-start | bytes 786440 | tf_op jit(solution)/shard_map/ppermute | solution.py:42
  53.5 16.0 %collective-permute-start.24 = (bf16[128,1024]{1,0:T(8,128)(2,1)S(1)}, bf16[128,1024]{1,0:T(8,128)(2,1)S(1)}, u32[]{:S(2)}, u32[]{:S(2)}) collective-permute-start(bf16[128,1024]{1,0:T(8,128)(2,1)S(1)} %bitcast.25), channel_id=1, source_target_pairs={{0,6},{2,0},{4,2},{6,4},{1,7},{3,1},{5,3},{7,5},{8,14},{10,8},{12,... | collective-permute-start | bytes 786440 | tf_op jit(solution)/shard_map/ppermute | solution.py:42
  53.8 25.6 %collective-permute-start.17 = (bf16[2,3,128,256]{3,2,1,0:T(8,128)(2,1)S(1)}, bf16[2,3,128,256]{3,2,1,0:T(8,128)(2,1)S(1)}, u32[]{:S(2)}, u32[]{:S(2)}) collective-permute-start(bf16[2,3,128,256]{3,2,1,0:T(8,128)(2,1)S(1)} %slice_bitcast_fusion.1), channel_id=1, source_target_pairs={{0,64},{8,24},{16,80},{24,40},{32,96},{40,56},{48,112},{56,8},{64,... | collective-permute-start | bytes 1179656 | tf_op jit(solution)/shard_map/ppermute | solution.py:506
  55.2 24.2 %collective-permute-start.18 = (bf16[2,3,128,256]{3,2,1,0:T(8,128)(2,1)S(1)}, bf16[2,3,128,256]{3,2,1,0:T(8,128)(2,1)S(1)}, u32[]{:S(2)}, u32[]{:S(2)}) collective-permute-start(bf16[2,3,128,256]{3,2,1,0:T(8,128)(2,1)S(1)} %slice_bitcast_fusion), channel_id=1, source_target_pairs={{0,192},{8,56},{16,208},{24,8},{32,224},{40,24},{48,240},{56,40},{... | collective-permute-start | bytes 1179656 | tf_op jit(solution)/shard_map/ppermute | solution.py:506
  63.9 15.4 %collective-permute-start.19 = (bf16[1,3,128,256]{3,2,1,0:T(8,128)(2,1)S(1)}, bf16[1,3,128,256]{3,2,1,0:T(8,128)(2,1)S(1)}, u32[]{:S(2)}, u32[]{:S(2)}) collective-permute-start(bf16[1,3,128,256]{3,2,1,0:T(8,128)(2,1)S(1)} %slice.42), channel_id=1, source_target_pairs={{0,64},{8,24},{16,80},{24,40},{32,96},{40,56},{48,112},{56,8},{64,... | collective-permute-start | bytes 589832 | tf_op jit(solution)/shard_map/ppermute | solution.py:506
  69.5 9.8 %collective-permute-start.20 = (bf16[1,3,128,256]{3,2,1,0:T(8,128)(2,1)S(1)}, bf16[1,3,128,256]{3,2,1,0:T(8,128)(2,1)S(1)}, u32[]{:S(2)}, u32[]{:S(2)}) collective-permute-start(bf16[1,3,128,256]{3,2,1,0:T(8,128)(2,1)S(1)} %slice.43), channel_id=1, source_target_pairs={{0,192},{8,56},{16,208},{24,8},{32,224},{40,24},{48,240},{56,40},{... | collective-permute-start | bytes 589832 | tf_op jit(solution)/shard_map/ppermute | solution.py:506
  71.0 22.8 %collective-permute-start.25 = (f32[128,256]{1,0:T(8,128)S(1)}, f32[128,256]{1,0:T(8,128)S(1)}, u32[]{:S(2)}, u32[]{:S(2)}) collective-permute-start(f32[128,256]{1,0:T(8,128)S(1)} %get-tuple-element.49), channel_id=1, source_target_pairs={{0,8},{8,0},{16,24},{24,16},{32,40},{40,32},{48,56},{56,48},{64,72... | collective-permute-start | bytes 393224 | tf_op jit(solution)/shard_map/ppermute | solution.py:38
  115.6 12.9 %collective-permute-start.29 = (bf16[3,128,1024]{2,1,0:T(8,128)(2,1)S(1)}, bf16[3,128,1024]{2,1,0:T(8,128)(2,1)S(1)}, u32[]{:S(2)}, u32[]{:S(2)}) collective-permute-start(bf16[3,128,1024]{2,1,0:T(8,128)(2,1)S(1)} %get-tuple-element.60), channel_id=1, source_target_pairs={{0,8},{8,0},{16,24},{24,16},{32,40},{40,32},{48,56},{56,48},{64,72... | collective-permute-start | bytes 2359304 | tf_op jit(solution)/shard_map/ppermute | solution.py:38
  120.6 16.7 %collective-permute-start.27 = (bf16[128,1024]{1,0:T(8,128)(2,1)S(1)}, bf16[128,1024]{1,0:T(8,128)(2,1)S(1)}, u32[]{:S(2)}, u32[]{:S(2)}) collective-permute-start(bf16[128,1024]{1,0:T(8,128)(2,1)S(1)} %shard_map.84), channel_id=1, source_target_pairs={{0,4},{2,6},{4,0},{6,2},{1,5},{3,7},{5,1},{7,3},{8,12},{10,14},{12... | collective-permute-start | bytes 786440 | tf_op jit(solution)/shard_map/ppermute | solution.py:42
  121.3 31.6 %collective-permute-start.26 = (bf16[128,1024]{1,0:T(8,128)(2,1)S(1)}, bf16[128,1024]{1,0:T(8,128)(2,1)S(1)}, u32[]{:S(2)}, u32[]{:S(2)}) collective-permute-start(bf16[128,1024]{1,0:T(8,128)(2,1)S(1)} %get-tuple-element.53), channel_id=1, source_target_pairs={{0,2},{2,4},{4,6},{6,0},{1,3},{3,5},{5,7},{7,1},{8,10},{10,12},{12... | collective-permute-start | bytes 786440 | tf_op jit(solution)/shard_map/ppermute | solution.py:42
  125.9 28.2 %collective-permute-start.28 = (bf16[128,1024]{1,0:T(8,128)(2,1)S(1)}, bf16[128,1024]{1,0:T(8,128)(2,1)S(1)}, u32[]{:S(2)}, u32[]{:S(2)}) collective-permute-start(bf16[128,1024]{1,0:T(8,128)(2,1)S(1)} %get-tuple-element.54), channel_id=1, source_target_pairs={{0,6},{2,0},{4,2},{6,4},{1,7},{3,1},{5,3},{7,5},{8,14},{10,8},{12,... | collective-permute-start | bytes 786440 | tf_op jit(solution)/shard_map/ppermute | solution.py:42
  127.4 32.7 %collective-permute-start.33 = (bf16[128,1024]{1,0:T(8,128)(2,1)S(1)}, bf16[128,1024]{1,0:T(8,128)(2,1)S(1)}, u32[]{:S(2)}, u32[]{:S(2)}) collective-permute-start(bf16[128,1024]{1,0:T(8,128)(2,1)S(1)} %shard_map.88), channel_id=1, source_target_pairs={{0,4},{2,6},{4,0},{6,2},{1,5},{3,7},{5,1},{7,3},{8,12},{10,14},{12... | collective-permute-start | bytes 786440 | tf_op jit(solution)/shard_map/ppermute | solution.py:42
  128.9 40.3 %collective-permute-start.31 = (bf16[128,1024]{1,0:T(8,128)(2,1)S(1)}, bf16[128,1024]{1,0:T(8,128)(2,1)S(1)}, u32[]{:S(2)}, u32[]{:S(2)}) collective-permute-start(bf16[128,1024]{1,0:T(8,128)(2,1)S(1)} %get-tuple-element.64), channel_id=1, source_target_pairs={{0,2},{2,4},{4,6},{6,0},{1,3},{3,5},{5,7},{7,1},{8,10},{10,12},{12... | collective-permute-start | bytes 786440 | tf_op jit(solution)/shard_map/ppermute | solution.py:42
  137.3 31.9 %collective-permute-start.34 = (bf16[128,1024]{1,0:T(8,128)(2,1)S(1)}, bf16[128,1024]{1,0:T(8,128)(2,1)S(1)}, u32[]{:S(2)}, u32[]{:S(2)}) collective-permute-start(bf16[128,1024]{1,0:T(8,128)(2,1)S(1)} %get-tuple-element.67), channel_id=1, source_target_pairs={{0,6},{2,0},{4,2},{6,4},{1,7},{3,1},{5,3},{7,5},{8,14},{10,8},{12,... | collective-permute-start | bytes 786440 | tf_op jit(solution)/shard_map/ppermute | solution.py:42
  (13 other events, 177.4 us)
